TPU v7x, 32 devices: a whole 2x2x4 slice. The times are simulated.
32 devices in a mesh: gz: 8 (over z, x), gy: 4 (over y, core).
Axes of the slice: x: 2, y: 2, z: 4, core: 2. Of those that a mesh axis runs over, the one named last changes fastest.
Arguments:
- features: bfloat16 [128, 64, 32, 128], P('gz', 'gy'), may hold values from -6 to 6
- occupancy: int32 [8, 4, 4], P('gz', 'gy'), may hold values from 0 to 1, as said below
- kernel: bfloat16 [3, 3, 3, 64, 128], replicated, may hold values from -0.15625 to 0.15625
- upstream: bfloat16 [64, 32, 32, 128], P('gz', 'gy'), may hold values from -6 to 6
Outputs:
- coarse: bfloat16 [64, 32, 32, 128], P('gz', 'gy')
- feature_grad: bfloat16 [128, 64, 32, 128], P('gz', 'gy')
- kernel_grad: float32 [3, 3, 3, 64, 128], replicated
Inputs may be any that keep to these rules, and one draw needn't show every extreme that they name: `occupancy`: each owner of 1 x 1 x 4 blocks holds at least one occupied block; owners' blocks are occupied at their own rates, so occupied counts differ between devices.
All inputs are finite; a program needn't handle non-finite values.
Results may differ from a plain program's by a relative error of at most 0.0022.
Values may be sent and summed in bfloat16 or wider, within the bound.
No kernel may reach another device: no remote copies, remote signals or barrier semaphores. Data moves between devices by JAX's collectives and lax.ppermute only.
A program may use at most 128 MiB of HBM per device.

v0:
```python
import functools

import jax
import jax.numpy as jnp
from jax import lax
from jax.experimental import pallas as pl
from jax.experimental.pallas import tpu as pltpu
from jax.sharding import PartitionSpec as P

F32 = jnp.float32
BF16 = jnp.bfloat16

TAPS = ((1, 1), (1, 2), (2, 1), (2, 2), (1, 0), (2, 0), (0, 1), (0, 2), (0, 0))


def row_mask(occ_ref, pairs, lanes):
    width = pairs // occ_ref.shape[2]
    block = lax.broadcasted_iota(jnp.int32, (pairs, lanes), 0) // width
    mask = jnp.zeros((pairs, lanes), F32)
    for k in range(occ_ref.shape[2]):
        here = occ_ref[0, 0, k].astype(F32)
        mask = jnp.where(block == k, here, mask)
    return mask


def with_next(g):
    pairs = g.shape[-2]
    axis = g.ndim - 2
    wide = pltpu.roll(g.astype(F32), pairs - 1, axis)
    last = lax.broadcasted_iota(jnp.int32, wide.shape, axis) == pairs - 1
    return jnp.concatenate([g, jnp.where(last, 0.0, wide).astype(BF16)], -1)


def fill_grads(gext, g_ref, gz_ref, gy_ref, occ_ref):
    zo, yo, pairs, cout = g_ref.shape
    mask = row_mask(occ_ref, pairs, cout).astype(BF16)
    for a in range(zo):
        gext[a, :yo] = with_next(g_ref[a] * mask)
    gext[zo, :yo] = with_next(gz_ref[...])
    gext[:, yo] = with_next(gy_ref[...])


def grad_rows(gext, a0, na, da, db):
    _, yo1, pairs, wide = gext.shape
    yo = yo1 - 1
    return gext[pl.ds(a0 + da, na), db : db + yo].reshape(na * yo * pairs, wide)


def fill_taps(taps, k_ref):
    cin, cout = k_ref.shape[1:]
    for s, (kz, ky) in enumerate(TAPS):
        t = 3 * (3 * kz + ky)
        r = s * 2 * cin
        taps[r : r + 2 * cin, :cout] = k_ref[t + 1 : t + 3].reshape(2 * cin, cout)
        taps[r : r + cin, cout:] = jnp.zeros((cin, cout), BF16)
        taps[r + cin : r + 2 * cin, cout:] = k_ref[t]


def weight_kernel(occ_ref, f_ref, g_ref, gz_ref, gy_ref, keep_ref, send_ref, gext, acc, flat):
    step = pl.program_id(0)
    na, _, yo, _, pairs, chans = f_ref.shape
    cin = chans // 2
    cout = g_ref.shape[3]

    @pl.when(step == 0)
    def _():
        fill_grads(gext, g_ref, gz_ref, gy_ref, occ_ref)
        acc[...] = jnp.zeros_like(acc)

    mask = row_mask(occ_ref, pairs, chans).astype(BF16)

    def rows(pz, py):
        return (f_ref[:, pz, :, py] * mask).reshape(na * yo * pairs, chans)

    ee, eo, oe, oo = rows(0, 0), rows(0, 1), rows(1, 0), rows(1, 1)
    a0 = step * na

    def product(x, da, db):
        g = grad_rows(gext, a0, na, da, db)
        return lax.dot_general(x, g, (((0,), (0,)), ((), ())), preferred_element_type=F32)

    c = chans
    acc[: 4 * c] += product(jnp.concatenate([ee, eo, oe, oo], 1), 0, 0)
    acc[4 * c : 6 * c] += product(jnp.concatenate([eo, oo], 1), 0, 1)
    acc[6 * c : 8 * c] += product(jnp.concatenate([oe, oo], 1), 1, 0)
    acc[8 * c : 9 * c] += product(oo, 1, 1)

    @pl.when(step == pl.num_programs(0) - 1)
    def _():
        for s, (kz, ky) in enumerate(TAPS):
            t = 3 * (3 * kz + ky) * cin
            r = s * chans
            flat[t : t + cin] = acc[r + cin : r + chans, cout:]
            flat[t + cin : t + 3 * cin] = acc[r : r + chans, :cout]
        half = keep_ref.shape[0]
        bit = lax.axis_index("gy") % 2
        keep_ref[...] = flat[pl.ds(pl.multiple_of(bit * half, 8), half)]
        send_ref[...] = flat[pl.ds(pl.multiple_of((1 - bit) * half, 8), half)]


def data_kernel(occ_ref, k_ref, g_ref, gz_ref, gy_ref, out_ref, gext, taps):
    step = pl.program_id(0)
    na, _, yo, _, pairs, chans = out_ref.shape

    @pl.when(step == 0)
    def _():
        fill_grads(gext, g_ref, gz_ref, gy_ref, occ_ref)
        fill_taps(taps, k_ref)

    a0 = step * na
    c = chans

    def product(da, db, first, count):
        g = grad_rows(gext, a0, na, da, db)
        w = taps[first * c : (first + count) * c]
        return lax.dot_general(g, w, (((1,), (1,)), ((), ())), preferred_element_type=F32)

    mask = row_mask(occ_ref, pairs, chans)
    p00 = product(0, 0, 0, 4)
    p01 = product(0, 1, 4, 2)
    p10 = product(1, 0, 6, 2)
    p11 = product(1, 1, 8, 1)

    def put(pz, py, value):
        out_ref[:, pz, :, py] = (value.reshape(na, yo, pairs, chans) * mask).astype(BF16)

    put(0, 0, p00[:, :c])
    put(0, 1, p00[:, c : 2 * c] + p01[:, :c])
    put(1, 0, p00[:, 2 * c : 3 * c] + p10[:, :c])
    put(1, 1, (p00[:, 3 * c :] + p01[:, c:]) + (p10[:, c:] + p11))


def coarse_kernel(occ_ref, k_ref, f_ref, fz_ref, fy_ref, out_ref, prev, taps):
    step = pl.program_id(0)
    na, _, yo, _, pairs, chans = f_ref.shape
    cout = out_ref.shape[3]

    @pl.when(step == 0)
    def _():
        fill_taps(taps, k_ref)
        prev[...] = fz_ref[...]

    mask = row_mask(occ_ref, pairs, chans).astype(BF16)
    even = f_ref[:, 0] * mask
    odd = f_ref[:, 1] * mask
    before = prev[...][None]
    if na > 1:
        before = jnp.concatenate([before, odd[:-1]], 0)
    prev[...] = odd[na - 1]
    z0 = 2 * na * step
    fy = fy_ref[pl.ds(z0, 2 * na + 1)]

    def rows(planes, rim, ky):
        if ky == 1:
            x = planes[:, :, 0]
        elif ky == 2:
            x = planes[:, :, 1]
        else:
            x = jnp.concatenate([rim[:, None], planes[:, :-1, 1]], 1)
        return x.reshape(na * yo * pairs, chans)

    rims = fy[1:].reshape(na, 2, pairs, chans)
    edge = fy[: 2 * na].reshape(na, 2, pairs, chans)
    planes = {0: (before, edge[:, 0]), 1: (even, rims[:, 0]), 2: (odd, rims[:, 1])}
    lhs = jnp.concatenate([rows(*planes[kz], ky) for kz, ky in TAPS], 1)
    both = jnp.dot(lhs, taps[...], preferred_element_type=F32)
    both = both.reshape(na * yo, pairs, 2 * cout)
    later = pltpu.roll(both[..., cout:], 1, 1)
    first = lax.broadcasted_iota(jnp.int32, later.shape, 1) == 0
    total = both[..., :cout] + jnp.where(first, 0.0, later)
    out = total * row_mask(occ_ref, pairs, cout)
    out_ref[...] = out.reshape(na, yo, pairs, cout).astype(BF16)


def whole(shape):
    return pl.BlockSpec(shape, lambda i: (0,) * len(shape))


def leading(shape, n):
    block = (n,) + tuple(shape[1:])
    return pl.BlockSpec(block, lambda i: (i,) + (0,) * (len(shape) - 1))


SCALARS = pl.BlockSpec(memory_space=pltpu.SMEM)
PARAMS = pltpu.CompilerParams(dimension_semantics=("arbitrary",), vmem_limit_bytes=40 << 20)


def cost(flops, nbytes):
    return pl.CostEstimate(flops=int(flops), bytes_accessed=int(nbytes), transcendentals=0)


def weight_grad(occ, split, grad, gz, gy, cin, na=2):
    zo, yo, pairs, cout = grad.shape
    chans = 2 * cin
    half = 27 * cin // 2
    part = jax.ShapeDtypeStruct((half, cout), F32)
    return pl.pallas_call(
        weight_kernel,
        grid=(zo // na,),
        in_specs=[SCALARS, leading(split.shape, na), whole(grad.shape), whole(gz.shape), whole(gy.shape)],
        out_specs=[whole(part.shape)] * 2,
        out_shape=[part, part],
        scratch_shapes=[
            pltpu.VMEM((zo + 1, yo + 1, pairs, 2 * cout), BF16),
            pltpu.VMEM((9 * chans, 2 * cout), F32),
            pltpu.VMEM((2 * half, cout), F32),
        ],
        compiler_params=PARAMS,
        cost_estimate=cost(2 * zo * yo * pairs * 9 * chans * 2 * cout, 2 * split.size),
    )(occ, split, grad, gz, gy)


def data_grad(occ, kernel, grad, gz, gy, na=1):
    zo, yo, pairs, cout = grad.shape
    cin = kernel.shape[1]
    chans = 2 * cin
    shape = (zo, 2, yo, 2, pairs, chans)
    return pl.pallas_call(
        data_kernel,
        grid=(zo // na,),
        in_specs=[SCALARS, whole(kernel.shape), whole(grad.shape), whole(gz.shape), whole(gy.shape)],
        out_specs=leading(shape, na),
        out_shape=jax.ShapeDtypeStruct(shape, BF16),
        scratch_shapes=[
            pltpu.VMEM((zo + 1, yo + 1, pairs, 2 * cout), BF16),
            pltpu.VMEM((9 * chans, 2 * cout), BF16),
        ],
        compiler_params=PARAMS,
        cost_estimate=cost(2 * zo * yo * pairs * 9 * chans * 2 * cout, 2 * zo * yo * pairs * 4 * chans),
    )(occ, kernel, grad, gz, gy)


def coarse_conv(occ, kernel, split, fz, fy, na=2):
    zo, _, yo, _, pairs, chans = split.shape
    cout = kernel.shape[2]
    shape = (zo, yo, pairs, cout)
    return pl.pallas_call(
        coarse_kernel,
        grid=(zo // na,),
        in_specs=[SCALARS, whole(kernel.shape), leading(split.shape, na), whole(fz.shape), whole(fy.shape)],
        out_specs=leading(shape, na),
        out_shape=jax.ShapeDtypeStruct(shape, BF16),
        scratch_shapes=[
            pltpu.VMEM((yo, 2, pairs, chans), BF16),
            pltpu.VMEM((9 * chans, 2 * cout), BF16),
        ],
        compiler_params=PARAMS,
        cost_estimate=cost(2 * zo * yo * pairs * 9 * chans * 2 * cout, 2 * split.size),
    )(occ, kernel, split, fz, fy)


def shifted(block, axis, distance):
    n = lax.axis_size(axis)
    return lax.ppermute(block, axis, [(i, i + distance) for i in range(n) if 0 <= i + distance < n])


def partners(nz, ny, other):
    moves = []
    for z in range(nz):
        for y in range(ny):
            pz, py = other(z, y)
            moves.append((z * ny + y, pz * ny + py))
    return moves


def join_kernel(a_ref, b_ref, c_ref, d_ref, out_ref, *, nz, ny):
    z, y = lax.axis_index("gz"), lax.axis_index("gy")
    core = y % 2
    up, along = (y // 2) % 2, z % 2
    first = jnp.where(core == 0, along, up)
    second = jnp.where(core == 0, up, along)
    part = a_ref.shape[0]

    def put(c, f, s, value):
        at = pl.multiple_of(((c * 2 + f) * 2 + s) * part, 8)
        out_ref[pl.ds(at, part)] = value.astype(F32)

    put(core, first, second, a_ref[...])
    put(core, first, 1 - second, b_ref[...])
    put(core, 1 - first, second, c_ref[:part])
    put(core, 1 - first, 1 - second, c_ref[part:])
    put(1 - core, second, first, d_ref[:part])
    put(1 - core, second, 1 - first, d_ref[part : 2 * part])
    put(1 - core, 1 - second, first, d_ref[2 * part : 3 * part])
    put(1 - core, 1 - second, 1 - first, d_ref[3 * part :])


def summed(keep, send):
    both = ("gz", "gy")
    nz, ny = lax.axis_size("gz"), lax.axis_size("gy")
    z, y = lax.axis_index("gz"), lax.axis_index("gy")
    core, up, along = y % 2, (y // 2) % 2, z % 2
    first = jnp.where(core == 0, along, up)
    second = jnp.where(core == 0, up, along)

    to_core = partners(nz, ny, lambda z, y: (z, y ^ 1))
    to_first = partners(nz, ny, lambda z, y: (z ^ 1, y) if y % 2 == 0 else (z, y ^ 2))
    to_second = partners(nz, ny, lambda z, y: (z, y ^ 2) if y % 2 == 0 else (z ^ 1, y))

    def half(x, bit):
        n = x.shape[0] // 2
        return lax.dynamic_slice_in_dim(x, bit * n, n, 0)

    got = lax.ppermute(send, both, to_core)
    for route, bit in ((to_first, first), (to_second, second)):
        send = half(keep, 1 - bit) + half(got, 1 - bit)
        keep = half(keep, bit) + half(got, bit)
        got = lax.ppermute(send, both, route)
    total = keep + got
    step = 2
    while step < nz:
        total = total + lax.ppermute(total, both, partners(nz, ny, lambda z, y: (z ^ step, y)))
        step *= 2

    a = total.astype(BF16)
    b = lax.ppermute(a, both, to_second)
    ab = jnp.concatenate([a, b], 0)
    c = lax.ppermute(ab, both, to_first)
    d = lax.ppermute(jnp.concatenate([ab, c], 0), both, to_core)
    vmem = pl.BlockSpec(memory_space=pltpu.VMEM)
    return pl.pallas_call(
        functools.partial(join_kernel, nz=nz, ny=ny),
        in_specs=[vmem] * 4,
        out_specs=vmem,
        out_shape=jax.ShapeDtypeStruct((8 * a.shape[0], a.shape[1]), F32),
        compiler_params=pltpu.CompilerParams(vmem_limit_bytes=16 << 20),
        cost_estimate=cost(0, 8 * a.size * 6),
    )(a, b, c, d)


def shards(features, occupancy, kernel, upstream):
    nz, ny = lax.axis_size("gz"), lax.axis_size("gy")
    if ny != 4 or nz & (nz - 1) or occupancy.shape[:2] != (1, 1):
        raise ValueError("unsupported mesh")
    zi, yi, pairs, chans = features.shape
    zo, yo = zi // 2, yi // 2
    taps = kernel.reshape((27,) + kernel.shape[3:])
    split = features.reshape(zo, 2, yo, 2, pairs, chans)
    mask = jnp.repeat(occupancy[0, 0], pairs // occupancy.shape[2]).astype(BF16)[None, :, None]

    gz = shifted(upstream[0] * mask, "gz", -1)
    gy = shifted(jnp.concatenate([upstream[:, 0] * mask, gz[:1]], 0), "gy", -1)
    keep, send = weight_grad(occupancy, split, upstream, gz, gy, chans // 2)
    kernel_grad = summed(keep, send).reshape(kernel.shape)

    fz = shifted(features[-1] * mask, "gz", 1)
    fy = shifted(jnp.concatenate([fz[-1:], features[:, -1] * mask], 0), "gy", 1)
    coarse = coarse_conv(occupancy, taps, split, fz.reshape(yo, 2, pairs, chans), fy)
    feature_grad = data_grad(occupancy, taps, upstream, gz, gy).reshape(features.shape)
    return (coarse, feature_grad, kernel_grad)


def solution(mesh):
    return jax.shard_map(
        shards,
        mesh=mesh,
        in_specs=(P("gz", "gy", None, None), P("gz", "gy", None), P(), P("gz", "gy", None, None)),
        out_specs=(P("gz", "gy", None, None), P("gz", "gy", None, None), P()),
        check_vma=False,
    )
```

profile of v0, /device:TPU:0, one launch (start us, length us, event | category | flops | bytes accessed | tf_op | source)
XLA Modules:
  0.0 71.0 jit_solution(13175140180826317866)
XLA Ops:
  0.6 0.7 convert_bitcast_fusion
  1.5 1.0 %bitcast_multiply_fusion.2 = (bf16[8,32,128]{2,1,0:T(8,128)(2,1)S(1)}, bf16[8,32,128]{2,1,0:T(8,128)(2,1)S(1)}) fusion(bf16[8,8,32,128]{3,2,1,0:T(8,128)(2,1)} %g_ref.3, bf16[32]{0:T(256)(128)(2,1)S(1)} %convert_element_type.19), kind=kLoop, calls=%fused_computation.11 | loop fusion | flops 65536 | bytes 262208 | tf_op jit(solution)/shard_map/mul | solution.py:342
  2.5 1.3 %collective-permute-start.2 = (bf16[8,32,128]{2,1,0:T(8,128)(2,1)S(1)}, bf16[8,32,128]{2,1,0:T(8,128)(2,1)S(1)}, u32[]{:S(2)}, u32[]{:S(2)}) collective-permute-start(bf16[8,32,128]{2,1,0:T(8,128)(2,1)S(1)} %get-tuple-element.12), channel_id=1, source_target_pairs={{4,0},{8,4},{12,8},{16,12},{20,16},{24,20},{28,24},{5,1},{9,5},{13... | collective-permute-start | bytes 196616 | tf_op jit(solution)/shard_map/ppermute | solution.py:254
  3.8 5.8 %collective-permute-done.2.gz_ref = bf16[8,32,128]{2,1,0:T(8,128)(2,1)S(1)} collective-permute-done((bf16[8,32,128]{2,1,0:T(8,128)(2,1)S(1)}, bf16[8,32,128]{2,1,0:T(8,128)(2,1)S(1)}, u32[]{:S(2)}, u32[]{:S(2)}) %collective-permute-start.2) | collective-permute-done | bytes 65568 | tf_op jit(solution)/shard_map/ppermute | solution.py:254
  9.6 1.3 %collective-permute-start.3 = (bf16[9,32,128]{2,1,0:T(8,128)(2,1)S(1)}, bf16[9,32,128]{2,1,0:T(8,128)(2,1)S(1)}, u32[]{:S(2)}, u32[]{:S(2)}) collective-permute-start(bf16[9,32,128]{2,1,0:T(8,128)(2,1)S(1)} %pad_maximum_fusion.3), channel_id=1, source_target_pairs={{1,0},{2,1},{3,2},{5,4},{6,5},{7,6},{9,8},{10,9},{11,10},{13,12},{... | collective-permute-start | bytes 221192 | tf_op jit(solution)/shard_map/ppermute | solution.py:254
  10.9 1.9 %collective-permute-done.3.gy_ref = bf16[9,32,128]{2,1,0:T(8,128)(2,1)S(1)} collective-permute-done((bf16[9,32,128]{2,1,0:T(8,128)(2,1)S(1)}, bf16[9,32,128]{2,1,0:T(8,128)(2,1)S(1)}, u32[]{:S(2)}, u32[]{:S(2)}) %collective-permute-start.3) | collective-permute-done | bytes 73760 | tf_op jit(solution)/shard_map/ppermute | solution.py:254
  12.7 1.6 %copy-done = bf16[16,16,32,128]{3,2,1,0:T(8,128)(2,1)S(1)} copy-done((bf16[16,16,32,128]{3,2,1,0:T(8,128)(2,1)S(1)}, bf16[16,16,32,128]{3,2,1,0:T(8,128)(2,1)}, u32[]{:S(2)}) %copy-start) | copy-done | bytes 2097176
  14.3 1.0 %copy-done.2 = bf16[8,8,32,128]{3,2,1,0:T(8,128)(2,1)S(1)} copy-done((bf16[8,8,32,128]{3,2,1,0:T(8,128)(2,1)S(1)}, bf16[8,8,32,128]{3,2,1,0:T(8,128)(2,1)}, u32[]{:S(2)}) %copy-start.2) | copy-done | bytes 524312
  15.4 0.7 copy-done.5
  16.0 3.2 %shard_map.69 = (f32[864,128]{1,0:T(8,128)S(1)}, f32[864,128]{1,0:T(8,128)S(1)}) custom-call(s32[1,1,4]{2,1,0:T(1,128)S(1)} %copy-done.5, bf16[8,2,8,2,32,128]{5,4,3,2,1,0:T(8,128)(2,1)S(1)} %bitcast.19, bf16[8,8,32,128]{3,2,1,0:T(8,128)(2,1)S(1)} %copy-done.2, bf16[8,32,128]{2,1,0:T(8,128)(2,1)S(1)} %collective-permute-done.2.gz_ref, ...), custom_call_target="tpu_custom_call" | custom-call | flops 1207959552 | bytes 2097152 | tf_op jit(solution)/shard_map/pallas_call | solution.py:197
  19.2 3.0 %collective-permute-start.4 = (f32[864,128]{1,0:T(8,128)S(1)}, f32[864,128]{1,0:T(8,128)}, u32[]{:S(2)}, u32[]{:S(2)}) collective-permute-start(f32[864,128]{1,0:T(8,128)S(1)} %get-tuple-element.6), channel_id=1, source_target_pairs={{0,1},{1,0},{2,3},{3,2},{4,5},{5,4},{6,7},{7,6},{8,9},{9,8},{10,11... | collective-permute-start | bytes 1327112 | tf_op jit(solution)/shard_map/ppermute | solution.py:304
  22.2 1.6 %collective-permute-done.4 = f32[864,128]{1,0:T(8,128)} collective-permute-done((f32[864,128]{1,0:T(8,128)S(1)}, f32[864,128]{1,0:T(8,128)}, u32[]{:S(2)}, u32[]{:S(2)}) %collective-permute-start.4) | collective-permute-done | bytes 442400 | tf_op jit(solution)/shard_map/ppermute | solution.py:304
  23.8 1.8 %dynamic-slice_add_fusion.1 = (f32[432,128]{1,0:T(8,128)S(1)}, f32[432,128]{1,0:T(8,128)}) fusion(f32[864,128]{1,0:T(8,128)} %collective-permute-done.4, s32[]{:T(128)S(6)} %select_n.46, f32[864,128]{1,0:T(8,128)S(1)} %get-tuple-element.5, s32[]{:T(128)S(6)} %select_n.49), kind=kLoop, calls=%fused_computation.2 | loop fusion | flops 110592 | bytes 1327112 | tf_op jit(solution)/shard_map/add | solution.py:307
  25.6 2.4 %collective-permute-start.5 = (f32[432,128]{1,0:T(8,128)}, f32[432,128]{1,0:T(8,128)}, u32[]{:S(2)}, u32[]{:S(2)}) collective-permute-start(f32[432,128]{1,0:T(8,128)} %get-tuple-element.10), channel_id=1, source_target_pairs={{0,4},{1,3},{2,6},{3,1},{4,0},{5,7},{6,2},{7,5},{8,12},{9,11},{10,... | collective-permute-start | bytes 663560 | tf_op jit(solution)/shard_map/ppermute | solution.py:308
  28.0 4.2 %collective-permute-done.5 = f32[432,128]{1,0:T(8,128)} collective-permute-done((f32[432,128]{1,0:T(8,128)}, f32[432,128]{1,0:T(8,128)}, u32[]{:S(2)}, u32[]{:S(2)}) %collective-permute-start.5) | collective-permute-done | bytes 221216 | tf_op jit(solution)/shard_map/ppermute | solution.py:308
  32.2 1.6 %dynamic-slice_add_fusion.2 = f32[216,128]{1,0:T(8,128)} fusion(f32[432,128]{1,0:T(8,128)} %collective-permute-done.5, s32[]{:T(128)S(6)} %select_n.50, f32[432,128]{1,0:T(8,128)S(1)} %get-tuple-element.9), kind=kLoop, calls=%fused_computation.8 | loop fusion | flops 27648 | bytes 331780 | tf_op jit(solution)/shard_map/add | solution.py:306
  33.8 0.2 collective-permute-start.6
  34.0 4.7 %collective-permute-done.6 = f32[216,128]{1,0:T(8,128)S(1)} collective-permute-done((f32[216,128]{1,0:T(8,128)}, f32[216,128]{1,0:T(8,128)S(1)}, u32[]{:S(2)}, u32[]{:S(2)}) %collective-permute-start.6) | collective-permute-done | bytes 110624 | tf_op jit(solution)/shard_map/ppermute | solution.py:308
  38.8 0.9 %add_add_fusion = f32[216,128]{1,0:T(8,128)S(1)} fusion(f32[216,128]{1,0:T(8,128)S(1)} %collective-permute-done.6, f32[432,128]{1,0:T(8,128)} %collective-permute-done.5, s32[]{:T(128)S(6)} %select_n.48, f32[432,128]{1,0:T(8,128)S(1)} %get-tuple-element.9), kind=kLoop, calls=%fused_computation.9 | loop fusion | flops 55296 | bytes 442372 | tf_op jit(solution)/shard_map/add | solution.py:309
  39.7 1.6 %collective-permute-start.7 = (f32[216,128]{1,0:T(8,128)S(1)}, f32[216,128]{1,0:T(8,128)S(1)}, u32[]{:S(2)}, u32[]{:S(2)}) collective-permute-start(f32[216,128]{1,0:T(8,128)S(1)} %add_add_fusion), channel_id=1, source_target_pairs={{0,8},{1,9},{2,10},{3,11},{4,12},{5,13},{6,14},{7,15},{8,0},{9,1},... | collective-permute-start | bytes 331784 | tf_op jit(solution)/shard_map/ppermute | solution.py:312
  41.3 3.2 %collective-permute-done.7 = f32[216,128]{1,0:T(8,128)S(1)} collective-permute-done((f32[216,128]{1,0:T(8,128)S(1)}, f32[216,128]{1,0:T(8,128)S(1)}, u32[]{:S(2)}, u32[]{:S(2)}) %collective-permute-start.7) | collective-permute-done | bytes 110624 | tf_op jit(solution)/shard_map/ppermute | solution.py:312
  44.5 2.7 %collective-permute-start.8 = (f32[216,128]{1,0:T(8,128)S(1)}, f32[216,128]{1,0:T(8,128)S(1)}, u32[]{:S(2)}, u32[]{:S(2)}) collective-permute-start(f32[216,128]{1,0:T(8,128)S(1)} %add.60), channel_id=1, source_target_pairs={{0,16},{1,17},{2,18},{3,19},{4,20},{5,21},{6,22},{7,23},{8,24},{9,... | collective-permute-start | bytes 331784 | tf_op jit(solution)/shard_map/ppermute | solution.py:312
  47.3 4.1 %collective-permute-start = (bf16[16,32,128]{2,1,0:T(8,128)(2,1)S(1)}, bf16[16,32,128]{2,1,0:T(8,128)(2,1)S(1)}, u32[]{:S(2)}, u32[]{:S(2)}) collective-permute-start(bf16[16,32,128]{2,1,0:T(8,128)(2,1)S(1)} %get-tuple-element.8), channel_id=1, source_target_pairs={{0,4},{4,8},{8,12},{12,16},{16,20},{20,24},{24,28},{1,5},{5,9},{9,... | collective-permute-start | bytes 393224 | tf_op jit(solution)/shard_map/ppermute | solution.py:254
  51.5 0.3 collective-permute-start.9
  51.7 2.2 %collective-permute-done = bf16[16,32,128]{2,1,0:T(8,128)(2,1)S(1)} collective-permute-done((bf16[16,32,128]{2,1,0:T(8,128)(2,1)S(1)}, bf16[16,32,128]{2,1,0:T(8,128)(2,1)S(1)}, u32[]{:S(2)}, u32[]{:S(2)}) %collective-permute-start) | collective-permute-done | bytes 131104 | tf_op jit(solution)/shard_map/ppermute | solution.py:254
  53.9 2.0 %collective-permute-done.9.b_ref = bf16[216,128]{1,0:T(8,128)(2,1)S(1)} collective-permute-done((bf16[216,128]{1,0:T(8,128)(2,1)S(1)}, bf16[216,128]{1,0:T(8,128)(2,1)S(1)}, u32[]{:S(2)}, u32[]{:S(2)}) %collective-permute-start.9) | collective-permute-done | bytes 55328 | tf_op jit(solution)/shard_map/ppermute | solution.py:316
  55.9 1.8 %collective-permute-start.10 = (bf16[432,128]{1,0:T(8,128)(2,1)S(1)}, bf16[432,128]{1,0:T(8,128)(2,1)S(1)}, u32[]{:S(2)}, u32[]{:S(2)}) collective-permute-start(bf16[432,128]{1,0:T(8,128)(2,1)S(1)} %pad_maximum_fusion.2), channel_id=1, source_target_pairs={{0,4},{1,3},{2,6},{3,1},{4,0},{5,7},{6,2},{7,5},{8,12},{9,11},{10,... | collective-permute-start | bytes 331784 | tf_op jit(solution)/shard_map/ppermute | solution.py:318
  57.8 1.3 %collective-permute-start.1 = (bf16[17,32,128]{2,1,0:T(8,128)(2,1)S(1)}, bf16[17,32,128]{2,1,0:T(8,128)(2,1)S(1)}, u32[]{:S(2)}, u32[]{:S(2)}) collective-permute-start(bf16[17,32,128]{2,1,0:T(8,128)(2,1)S(1)} %pad_maximum_fusion.1), channel_id=1, source_target_pairs={{0,1},{1,2},{2,3},{4,5},{5,6},{6,7},{8,9},{9,10},{10,11},{12,13},{... | collective-permute-start | bytes 417800 | tf_op jit(solution)/shard_map/ppermute | solution.py:254
  59.1 1.7 %collective-permute-done.10.c_ref = bf16[432,128]{1,0:T(8,128)(2,1)S(1)} collective-permute-done((bf16[432,128]{1,0:T(8,128)(2,1)S(1)}, bf16[432,128]{1,0:T(8,128)(2,1)S(1)}, u32[]{:S(2)}, u32[]{:S(2)}) %collective-permute-start.10) | collective-permute-done | bytes 110624 | tf_op jit(solution)/shard_map/ppermute | solution.py:318
  60.9 5.6 %shard_map.68 = bf16[8,2,8,2,32,128]{5,4,3,2,1,0:T(8,128)(2,1)} custom-call(s32[1,1,4]{2,1,0:T(1,128)S(1)} %copy-done.6, bf16[27,64,128]{2,1,0:T(8,128)(2,1)S(1)} %bitcast.22, bf16[8,8,32,128]{3,2,1,0:T(8,128)(2,1)S(1)} %copy-done.3, bf16[8,32,128]{2,1,0:T(8,128)(2,1)S(1)} %collective-permute-done.2.gz_ref, bf16[9,32,128]{2,1,0:T(8,128)(2,1)S(1)} %collective-permute-done.3.gy_ref), custom_call_target="tpu_custom_call" | custom-call | flops 1207959552 | bytes 2097152 | tf_op jit(solution)/shard_map/pallas_call | solution.py:218
  66.5 3.5 %shard_map.67 = bf16[8,8,32,128]{3,2,1,0:T(8,128)(2,1)} custom-call(s32[1,1,4]{2,1,0:T(1,128)S(1)} %copy-done.6, bf16[27,64,128]{2,1,0:T(8,128)(2,1)S(1)} %bitcast.23, bf16[8,2,8,2,32,128]{5,4,3,2,1,0:T(8,128)(2,1)S(1)} %bitcast.20, bf16[8,2,32,128]{3,2,1,0:T(8,128)(2,1)S(1)} %bitcast.21, bf16[17,32,128]{2,1,0:T(8,128)(2,1)S(1)} %collective-permute-done.1.fy_ref), custom_call_target="tpu_custom_call" | custom-call | flops 1207959552 | bytes 2097152 | tf_op jit(solution)/shard_map/pallas_call | solution.py:237
  70.0 1.0 %shard_map.70 = f32[1728,128]{1,0:T(8,128)} custom-call(bf16[216,128]{1,0:T(8,128)(2,1)S(1)} %add_convert_fusion.a_ref, bf16[216,128]{1,0:T(8,128)(2,1)S(1)} %collective-permute-done.9.b_ref, bf16[432,128]{1,0:T(8,128)(2,1)S(1)} %collective-permute-done.10.c_ref, bf16[864,128]{1,0:T(8,128)(2,1)S(1)} %collective-permute-done.11.d_ref), custom_call_target="tpu_custom_call" | custom-call | bytes 1327104 | tf_op jit(solution)/shard_map/pallas_call | solution.py:321
  (26 shorter events, 0.4 us)
Async XLA Ops:
  2.5 7.1 %collective-permute-start.2 = (bf16[8,32,128]{2,1,0:T(8,128)(2,1)S(1)}, bf16[8,32,128]{2,1,0:T(8,128)(2,1)S(1)}, u32[]{:S(2)}, u32[]{:S(2)}) collective-permute-start(bf16[8,32,128]{2,1,0:T(8,128)(2,1)S(1)} %get-tuple-element.12), channel_id=1, source_target_pairs={{4,0},{8,4},{12,8},{16,12},{20,16},{24,20},{28,24},{5,1},{9,5},{13... | collective-permute-start | bytes 196616 | tf_op jit(solution)/shard_map/ppermute | solution.py:254
  9.6 3.2 %collective-permute-start.3 = (bf16[9,32,128]{2,1,0:T(8,128)(2,1)S(1)}, bf16[9,32,128]{2,1,0:T(8,128)(2,1)S(1)}, u32[]{:S(2)}, u32[]{:S(2)}) collective-permute-start(bf16[9,32,128]{2,1,0:T(8,128)(2,1)S(1)} %pad_maximum_fusion.3), channel_id=1, source_target_pairs={{1,0},{2,1},{3,2},{5,4},{6,5},{7,6},{9,8},{10,9},{11,10},{13,12},{... | collective-permute-start | bytes 221192 | tf_op jit(solution)/shard_map/ppermute | solution.py:254
  12.7 1.6 %copy-start = (bf16[16,16,32,128]{3,2,1,0:T(8,128)(2,1)S(1)}, bf16[16,16,32,128]{3,2,1,0:T(8,128)(2,1)}, u32[]{:S(2)}) copy-start(bf16[16,16,32,128]{3,2,1,0:T(8,128)(2,1)} %param.4) | copy-start | bytes 6291460
  14.3 1.0 %copy-start.2 = (bf16[8,8,32,128]{3,2,1,0:T(8,128)(2,1)S(1)}, bf16[8,8,32,128]{3,2,1,0:T(8,128)(2,1)}, u32[]{:S(2)}) copy-start(bf16[8,8,32,128]{3,2,1,0:T(8,128)(2,1)} %g_ref.3) | copy-start | bytes 1572868
  15.4 0.7 copy-start.5
  19.2 27.9 %copy-start.1 = (bf16[16,16,32,128]{3,2,1,0:T(8,128)(2,1)S(1)}, bf16[16,16,32,128]{3,2,1,0:T(8,128)(2,1)}, u32[]{:S(2)}) copy-start(bf16[16,16,32,128]{3,2,1,0:T(8,128)(2,1)} %param.4) | copy-start | bytes 6291460
  19.2 4.6 %collective-permute-start.4 = (f32[864,128]{1,0:T(8,128)S(1)}, f32[864,128]{1,0:T(8,128)}, u32[]{:S(2)}, u32[]{:S(2)}) collective-permute-start(f32[864,128]{1,0:T(8,128)S(1)} %get-tuple-element.6), channel_id=1, source_target_pairs={{0,1},{1,0},{2,3},{3,2},{4,5},{5,4},{6,7},{7,6},{8,9},{9,8},{10,11... | collective-permute-start | bytes 1327112 | tf_op jit(solution)/shard_map/ppermute | solution.py:304
  23.8 37.0 %copy-start.3 = (bf16[8,8,32,128]{3,2,1,0:T(8,128)(2,1)S(1)}, bf16[8,8,32,128]{3,2,1,0:T(8,128)(2,1)}, u32[]{:S(2)}) copy-start(bf16[8,8,32,128]{3,2,1,0:T(8,128)(2,1)} %g_ref.3) | copy-start | bytes 1572868
  23.8 37.1 %copy-start.6 = (s32[1,1,4]{2,1,0:T(1,128)S(1)}, s32[1,1,4]{2,1,0:T(1,128)}, u32[]{:S(2)}) copy-start(s32[1,1,4]{2,1,0:T(1,128)} %occ_ref.5) | copy-start | bytes 52
  25.6 35.2 %copy-start.4 = (bf16[3,3,3,64,128]{4,3,2,1,0:T(8,128)(2,1)S(1)}, bf16[3,3,3,64,128]{4,3,2,1,0:T(8,128)(2,1)}, u32[]{:S(2)}) copy-start(bf16[3,3,3,64,128]{4,3,2,1,0:T(8,128)(2,1)} %param.6) | copy-start | bytes 1327108
  25.6 6.6 %collective-permute-start.5 = (f32[432,128]{1,0:T(8,128)}, f32[432,128]{1,0:T(8,128)}, u32[]{:S(2)}, u32[]{:S(2)}) collective-permute-start(f32[432,128]{1,0:T(8,128)} %get-tuple-element.10), channel_id=1, source_target_pairs={{0,4},{1,3},{2,6},{3,1},{4,0},{5,7},{6,2},{7,5},{8,12},{9,11},{10,... | collective-permute-start | bytes 663560 | tf_op jit(solution)/shard_map/ppermute | solution.py:308
  33.8 5.0 %collective-permute-start.6 = (f32[216,128]{1,0:T(8,128)}, f32[216,128]{1,0:T(8,128)S(1)}, u32[]{:S(2)}, u32[]{:S(2)}) collective-permute-start(f32[216,128]{1,0:T(8,128)} %dynamic-slice_add_fusion.2), channel_id=1, source_target_pairs={{0,2},{1,5},{2,0},{3,7},{4,6},{5,1},{6,4},{7,3},{8,10},{9,13},{10,... | collective-permute-start | bytes 331784 | tf_op jit(solution)/shard_map/ppermute | solution.py:308
  39.7 4.8 %collective-permute-start.7 = (f32[216,128]{1,0:T(8,128)S(1)}, f32[216,128]{1,0:T(8,128)S(1)}, u32[]{:S(2)}, u32[]{:S(2)}) collective-permute-start(f32[216,128]{1,0:T(8,128)S(1)} %add_add_fusion), channel_id=1, source_target_pairs={{0,8},{1,9},{2,10},{3,11},{4,12},{5,13},{6,14},{7,15},{8,0},{9,1},... | collective-permute-start | bytes 331784 | tf_op jit(solution)/shard_map/ppermute | solution.py:312
  44.5 6.9 %collective-permute-start.8 = (f32[216,128]{1,0:T(8,128)S(1)}, f32[216,128]{1,0:T(8,128)S(1)}, u32[]{:S(2)}, u32[]{:S(2)}) collective-permute-start(f32[216,128]{1,0:T(8,128)S(1)} %add.60), channel_id=1, source_target_pairs={{0,16},{1,17},{2,18},{3,19},{4,20},{5,21},{6,22},{7,23},{8,24},{9,... | collective-permute-start | bytes 331784 | tf_op jit(solution)/shard_map/ppermute | solution.py:312
  47.3 6.6 %collective-permute-start = (bf16[16,32,128]{2,1,0:T(8,128)(2,1)S(1)}, bf16[16,32,128]{2,1,0:T(8,128)(2,1)S(1)}, u32[]{:S(2)}, u32[]{:S(2)}) collective-permute-start(bf16[16,32,128]{2,1,0:T(8,128)(2,1)S(1)} %get-tuple-element.8), channel_id=1, source_target_pairs={{0,4},{4,8},{8,12},{12,16},{16,20},{20,24},{24,28},{1,5},{5,9},{9,... | collective-permute-start | bytes 393224 | tf_op jit(solution)/shard_map/ppermute | solution.py:254
  51.5 4.5 %collective-permute-start.9 = (bf16[216,128]{1,0:T(8,128)(2,1)S(1)}, bf16[216,128]{1,0:T(8,128)(2,1)S(1)}, u32[]{:S(2)}, u32[]{:S(2)}) collective-permute-start(bf16[216,128]{1,0:T(8,128)(2,1)S(1)} %add_convert_fusion.a_ref), channel_id=1, source_target_pairs={{0,2},{1,5},{2,0},{3,7},{4,6},{5,1},{6,4},{7,3},{8,10},{9,13},{10,... | collective-permute-start | bytes 165896 | tf_op jit(solution)/shard_map/ppermute | solution.py:316
  55.9 4.8 %collective-permute-start.10 = (bf16[432,128]{1,0:T(8,128)(2,1)S(1)}, bf16[432,128]{1,0:T(8,128)(2,1)S(1)}, u32[]{:S(2)}, u32[]{:S(2)}) collective-permute-start(bf16[432,128]{1,0:T(8,128)(2,1)S(1)} %pad_maximum_fusion.2), channel_id=1, source_target_pairs={{0,4},{1,3},{2,6},{3,1},{4,0},{5,7},{6,2},{7,5},{8,12},{9,11},{10,... | collective-permute-start | bytes 331784 | tf_op jit(solution)/shard_map/ppermute | solution.py:318
  57.8 8.7 %collective-permute-start.1 = (bf16[17,32,128]{2,1,0:T(8,128)(2,1)S(1)}, bf16[17,32,128]{2,1,0:T(8,128)(2,1)S(1)}, u32[]{:S(2)}, u32[]{:S(2)}) collective-permute-start(bf16[17,32,128]{2,1,0:T(8,128)(2,1)S(1)} %pad_maximum_fusion.1), channel_id=1, source_target_pairs={{0,1},{1,2},{2,3},{4,5},{5,6},{6,7},{8,9},{9,10},{10,11},{12,13},{... | collective-permute-start | bytes 417800 | tf_op jit(solution)/shard_map/ppermute | solution.py:254
  60.8 9.2 %collective-permute-start.11 = (bf16[864,128]{1,0:T(8,128)(2,1)S(1)}, bf16[864,128]{1,0:T(8,128)(2,1)S(1)}, u32[]{:S(2)}, u32[]{:S(2)}) collective-permute-start(bf16[864,128]{1,0:T(8,128)(2,1)S(1)} %pad_maximum_fusion), channel_id=1, source_target_pairs={{0,1},{1,0},{2,3},{3,2},{4,5},{5,4},{6,7},{7,6},{8,9},{9,8},{10,11... | collective-permute-start | bytes 663560 | tf_op jit(solution)/shard_map/ppermute | solution.py:319
where the time goes:
time: 71.4 us; the launch traced here: 71 us
  waiting for transfers between devices  27.2 us (38%)
  starting transfers between devices  20.1 us (28%)
  Pallas kernels  13.3 us (19%)
  other arithmetic  6.14 us (9%)
  local copies, waits for them, and re-layouts  3.47 us (5%)
  between operations  0.77 us (1%)
    ppermute x4, waiting for transfers between devices, shifted(): lax.ppermute(block, axis, [(i, i + distance) for i in range(n) if 0 <= i...  9.88 us
    ppermute x2, waiting for transfers between devices, summed(): got = lax.ppermute(send, both, route)  8.97 us
    ppermute x4, starting transfers between devices, shifted(): lax.ppermute(block, axis, [(i, i + distance) for i in range(n) if 0 <= i...  8.02 us
    pallas_call x1, Pallas kernels, data_grad(): pl.pallas_call(data_kernel, grid=(zo // na,), in_specs=[SCALARS, whole(ke...  5.6 us
    ppermute x2, starting transfers between devices, summed(): lax.ppermute(total, both, partners(nz, ny, lambda z, y: (z ^ step, y)))  4.3 us
    pallas_call x1, Pallas kernels, coarse_conv(): pl.pallas_call(coarse_kernel, grid=(zo // na,), in_specs=[SCALARS, whole(...  3.53 us
    unnamed x14, local copies, waits for them, and re-layouts  3.3 us
    pallas_call x1, Pallas kernels, weight_grad(): pl.pallas_call(weight_kernel, grid=(zo // na,), in_specs=[SCALARS, leadin...  3.19 us
  transfers between devices with their start and end apart: 12, of which 9 were waited for; matrix products, arithmetic and copies ran while one was open for 0% of the time, Pallas kernels for 13%

commit v1 on v0

--- a/solution.py
+++ b/solution.py
@@ -1,11 +1,10 @@
-import functools
-
 import jax
 import jax.numpy as jnp
 from jax import lax
 from jax.experimental import pallas as pl
 from jax.experimental.pallas import tpu as pltpu
 from jax.sharding import PartitionSpec as P
+
 
 F32 = jnp.float32
 BF16 = jnp.bfloat16
@@ -36,8 +35,8 @@
     mask = row_mask(occ_ref, pairs, cout).astype(BF16)
     for a in range(zo):
         gext[a, :yo] = with_next(g_ref[a] * mask)
-    gext[zo, :yo] = with_next(gz_ref[...])
-    gext[:, yo] = with_next(gy_ref[...])
+    gext[:zo, yo] = with_next(gy_ref[...])
+    gext[zo] = with_next(gz_ref[...])
 
 
 def grad_rows(gext, a0, na, da, db):
@@ -56,16 +55,48 @@
         taps[r + cin : r + 2 * cin, cout:] = k_ref[t]
 
 
-def weight_kernel(occ_ref, f_ref, g_ref, gz_ref, gy_ref, keep_ref, send_ref, gext, acc, flat):
+def rims_of(occ, features, grad):
+    zi, yi, pairs, chans = features.shape
+    zo, yo, _, cout = grad.shape
+    sizes = ((yo, pairs, cout), (zo, pairs, cout), (yi, pairs, chans), (zi, pairs, chans))
+
+    def body(occ_ref, fl_ref, fb_ref, ga_ref, gb_ref, gz_ref, gy_ref, fz_ref, fy_ref):
+        mask = row_mask(occ_ref, pairs, chans).astype(BF16)
+        gz_ref[...] = ga_ref[0] * mask
+        gy_ref[...] = gb_ref[:, 0] * mask
+        fz_ref[...] = fl_ref[0] * mask
+        fy_ref[...] = fb_ref[:, 0] * mask
+
+    return pl.pallas_call(
+        body,
+        grid=(1,),
+        in_specs=[
+            SCALARS,
+            pl.BlockSpec((1, yi, pairs, chans), lambda i: (zi - 1, 0, 0, 0)),
+            pl.BlockSpec((zi, 1, pairs, chans), lambda i: (0, yi - 1, 0, 0)),
+            pl.BlockSpec((1, yo, pairs, cout), lambda i: (0, 0, 0, 0)),
+            pl.BlockSpec((zo, 1, pairs, cout), lambda i: (0, 0, 0, 0)),
+        ],
+        out_specs=[whole(x) for x in sizes],
+        out_shape=[jax.ShapeDtypeStruct(x, BF16) for x in sizes],
+        compiler_params=pltpu.CompilerParams(vmem_limit_bytes=4 << 20),
+        cost_estimate=cost(0, 2 * 2 * sum(x[0] * x[1] * x[2] for x in sizes)),
+    )(in_hbm(occ), in_hbm(features), in_hbm(features), in_hbm(grad), in_hbm(grad))
+
+
+def weight_kernel(occ_ref, f_ref, g_ref, acc_ref, gext):
     step = pl.program_id(0)
     na, _, yo, _, pairs, chans = f_ref.shape
-    cin = chans // 2
-    cout = g_ref.shape[3]
+    zo, _, _, cout = g_ref.shape
 
     @pl.when(step == 0)
     def _():
-        fill_grads(gext, g_ref, gz_ref, gy_ref, occ_ref)
-        acc[...] = jnp.zeros_like(acc)
+        mask = row_mask(occ_ref, pairs, cout).astype(BF16)
+        for a in range(zo):
+            gext[a, :yo] = with_next(g_ref[a] * mask)
+        gext[zo] = jnp.zeros(gext.shape[1:], BF16)
+        gext[:, yo] = jnp.zeros((zo + 1, pairs, 2 * cout), BF16)
+        acc_ref[...] = jnp.zeros_like(acc_ref)
 
     mask = row_mask(occ_ref, pairs, chans).astype(BF16)
 
@@ -74,28 +105,63 @@
 
     ee, eo, oe, oo = rows(0, 0), rows(0, 1), rows(1, 0), rows(1, 1)
     a0 = step * na
+    c = chans
 
     def product(x, da, db):
-        g = grad_rows(gext, a0, na, da, db)
-        return lax.dot_general(x, g, (((0,), (0,)), ((), ())), preferred_element_type=F32)
-
+        return rows_product(x, grad_rows(gext, a0, na, da, db))
+
+    acc_ref[: 4 * c] += product(jnp.concatenate([ee, eo, oe, oo], 1), 0, 0)
+    acc_ref[4 * c : 6 * c] += product(jnp.concatenate([eo, oo], 1), 0, 1)
+    acc_ref[6 * c : 8 * c] += product(jnp.concatenate([oe, oo], 1), 1, 0)
+    acc_ref[8 * c : 9 * c] += product(oo, 1, 1)
+
+
+def rows_product(x, g):
+    return lax.dot_general(x, g, (((0,), (0,)), ((), ())), preferred_element_type=F32)
+
+
+def place():
+    z, y = lax.axis_index("gz"), lax.axis_index("gy")
+    core, up, along = y % 2, (y // 2) % 2, z % 2
+    first = jnp.where(core == 0, along, up)
+    second = jnp.where(core == 0, up, along)
+    return core, first, second
+
+
+def edge_kernel(acc_ref, fz_ref, fy_ref, gz_ref, gy_ref, keep_ref, send_ref, acc, flat):
+    yi, pairs, chans = fz_ref.shape
+    cin, cout, yo, zo = chans // 2, gz_ref.shape[2], yi // 2, gy_ref.shape[0]
     c = chans
-    acc[: 4 * c] += product(jnp.concatenate([ee, eo, oe, oo], 1), 0, 0)
-    acc[4 * c : 6 * c] += product(jnp.concatenate([eo, oo], 1), 0, 1)
-    acc[6 * c : 8 * c] += product(jnp.concatenate([oe, oo], 1), 1, 0)
-    acc[8 * c : 9 * c] += product(oo, 1, 1)
-
-    @pl.when(step == pl.num_programs(0) - 1)
-    def _():
-        for s, (kz, ky) in enumerate(TAPS):
-            t = 3 * (3 * kz + ky) * cin
-            r = s * chans
-            flat[t : t + cin] = acc[r + cin : r + chans, cout:]
-            flat[t + cin : t + 3 * cin] = acc[r : r + chans, :cout]
-        half = keep_ref.shape[0]
-        bit = lax.axis_index("gy") % 2
-        keep_ref[...] = flat[pl.ds(pl.multiple_of(bit * half, 8), half)]
-        send_ref[...] = flat[pl.ds(pl.multiple_of((1 - bit) * half, 8), half)]
+    fz = fz_ref[...].reshape(yo, 2, pairs, chans)
+    fy = fy_ref[...].reshape(zo, 2, pairs, chans)
+    gz, gy = with_next(gz_ref[...]), with_next(gy_ref[...])
+
+    def flatten(x):
+        return x.reshape(x.shape[0] * pairs, x.shape[-1])
+
+    oe, oo = flatten(fz[:, 0]), flatten(fz[:, 1])
+    acc[6 * c : 8 * c] = acc_ref[6 * c : 8 * c] + rows_product(jnp.concatenate([oe, oo], 1), flatten(gz[:yo]))
+    last = rows_product(oo, flatten(gz[1:]))
+    eo, oo = flatten(fy[:, 0]), flatten(fy[:, 1])
+    acc[4 * c : 6 * c] = acc_ref[4 * c : 6 * c] + rows_product(jnp.concatenate([eo, oo], 1), flatten(gy))
+    last = last + rows_product(oo[: -pairs], flatten(gy[1:]))
+    acc[8 * c :] = acc_ref[8 * c :] + last
+
+    for s, (kz, ky) in enumerate(TAPS):
+        t = 3 * (3 * kz + ky) * cin
+        r = s * chans
+        source = acc_ref if s < 4 else acc
+        flat[t : t + cin] = source[r + cin : r + chans, cout:]
+        flat[t + cin : t + 3 * cin] = source[r : r + chans, :cout]
+    core, first, second = place()
+    part = keep_ref.shape[0] // 4
+    for f in range(2):
+        for s in range(2):
+            to = (2 * f + s) * part
+            mine = ((core * 2 + (first ^ f)) * 2 + (second ^ s)) * part
+            keep_ref[to : to + part] = flat[pl.ds(pl.multiple_of(mine, 8), part)]
+            its = (((1 - core) * 2 + (second ^ f)) * 2 + (first ^ s)) * part
+            send_ref[to : to + part] = flat[pl.ds(pl.multiple_of(its, 8), part)]
 
 
 def data_kernel(occ_ref, k_ref, g_ref, gz_ref, gy_ref, out_ref, gext, taps):
@@ -130,7 +196,7 @@
     put(1, 1, (p00[:, 3 * c :] + p01[:, c:]) + (p10[:, c:] + p11))
 
 
-def coarse_kernel(occ_ref, k_ref, f_ref, fz_ref, fy_ref, out_ref, prev, taps):
+def coarse_kernel(occ_ref, k_ref, f_ref, fz_ref, fy_ref, out_ref, prev, rim, taps):
     step = pl.program_id(0)
     na, _, yo, _, pairs, chans = f_ref.shape
     cout = out_ref.shape[3]
@@ -138,7 +204,9 @@
     @pl.when(step == 0)
     def _():
         fill_taps(taps, k_ref)
-        prev[...] = fz_ref[...]
+        prev[...] = fz_ref[1:].reshape(prev.shape)
+        rim[0] = fz_ref[0]
+        rim[1:] = fy_ref[...]
 
     mask = row_mask(occ_ref, pairs, chans).astype(BF16)
     even = f_ref[:, 0] * mask
@@ -148,15 +216,15 @@
         before = jnp.concatenate([before, odd[:-1]], 0)
     prev[...] = odd[na - 1]
     z0 = 2 * na * step
-    fy = fy_ref[pl.ds(z0, 2 * na + 1)]
-
-    def rows(planes, rim, ky):
+    fy = rim[pl.ds(z0, 2 * na + 1)]
+
+    def rows(planes, before, ky):
         if ky == 1:
             x = planes[:, :, 0]
         elif ky == 2:
             x = planes[:, :, 1]
         else:
-            x = jnp.concatenate([rim[:, None], planes[:, :-1, 1]], 1)
+            x = jnp.concatenate([before[:, None], planes[:, :-1, 1]], 1)
         return x.reshape(na * yo * pairs, chans)
 
     rims = fy[1:].reshape(na, 2, pairs, chans)
@@ -172,6 +240,10 @@
     out_ref[...] = out.reshape(na, yo, pairs, cout).astype(BF16)
 
 
+def in_hbm(x):
+    return pltpu.with_memory_space_constraint(x, pltpu.HBM)
+
+
 def whole(shape):
     return pl.BlockSpec(shape, lambda i: (0,) * len(shape))
 
@@ -182,32 +254,43 @@
 
 
 SCALARS = pl.BlockSpec(memory_space=pltpu.SMEM)
-PARAMS = pltpu.CompilerParams(dimension_semantics=("arbitrary",), vmem_limit_bytes=40 << 20)
+PARAMS = pltpu.CompilerParams(dimension_semantics=("arbitrary",), vmem_limit_bytes=16 << 20)
 
 
 def cost(flops, nbytes):
     return pl.CostEstimate(flops=int(flops), bytes_accessed=int(nbytes), transcendentals=0)
 
 
-def weight_grad(occ, split, grad, gz, gy, cin, na=2):
+def weight_grad(occ, split, grad, cin, na=2):
     zo, yo, pairs, cout = grad.shape
     chans = 2 * cin
+    shape = (9 * chans, 2 * cout)
+    return pl.pallas_call(
+        weight_kernel,
+        grid=(zo // na,),
+        in_specs=[SCALARS, leading(split.shape, na), whole(grad.shape)],
+        out_specs=whole(shape),
+        out_shape=jax.ShapeDtypeStruct(shape, F32),
+        scratch_shapes=[pltpu.VMEM((zo + 1, yo + 1, pairs, 2 * cout), BF16)],
+        compiler_params=PARAMS,
+        cost_estimate=cost(2 * zo * yo * pairs * 9 * chans * 2 * cout, 2 * split.size),
+    )(occ, split, grad)
+
+
+def with_edges(acc, fz, fy, gz, gy):
+    cin, cout = fz.shape[2] // 2, gz.shape[2]
     half = 27 * cin // 2
     part = jax.ShapeDtypeStruct((half, cout), F32)
-    return pl.pallas_call(
-        weight_kernel,
-        grid=(zo // na,),
-        in_specs=[SCALARS, leading(split.shape, na), whole(grad.shape), whole(gz.shape), whole(gy.shape)],
-        out_specs=[whole(part.shape)] * 2,
+    vmem = pl.BlockSpec(memory_space=pltpu.VMEM)
+    return pl.pallas_call(
+        edge_kernel,
+        in_specs=[vmem] * 5,
+        out_specs=[vmem] * 2,
         out_shape=[part, part],
-        scratch_shapes=[
-            pltpu.VMEM((zo + 1, yo + 1, pairs, 2 * cout), BF16),
-            pltpu.VMEM((9 * chans, 2 * cout), F32),
-            pltpu.VMEM((2 * half, cout), F32),
-        ],
-        compiler_params=PARAMS,
-        cost_estimate=cost(2 * zo * yo * pairs * 9 * chans * 2 * cout, 2 * split.size),
-    )(occ, split, grad, gz, gy)
+        scratch_shapes=[pltpu.VMEM(acc.shape, F32), pltpu.VMEM((2 * half, cout), F32)],
+        compiler_params=pltpu.CompilerParams(vmem_limit_bytes=12 << 20),
+        cost_estimate=cost(2 * 2 * 256 * 9 * fz.shape[2] * cout, 8 * acc.size),
+    )(acc, fz, fy, gz, gy)
 
 
 def data_grad(occ, kernel, grad, gz, gy, na=1):
@@ -242,6 +325,7 @@
         out_shape=jax.ShapeDtypeStruct(shape, BF16),
         scratch_shapes=[
             pltpu.VMEM((yo, 2, pairs, chans), BF16),
+            pltpu.VMEM((2 * zo + 1, pairs, chans), BF16),
             pltpu.VMEM((9 * chans, 2 * cout), BF16),
         ],
         compiler_params=PARAMS,
@@ -263,12 +347,8 @@
     return moves
 
 
-def join_kernel(a_ref, b_ref, c_ref, d_ref, out_ref, *, nz, ny):
-    z, y = lax.axis_index("gz"), lax.axis_index("gy")
-    core = y % 2
-    up, along = (y // 2) % 2, z % 2
-    first = jnp.where(core == 0, along, up)
-    second = jnp.where(core == 0, up, along)
+def join_kernel(a_ref, b_ref, c_ref, d_ref, out_ref):
+    core, first, second = place()
     part = a_ref.shape[0]
 
     def put(c, f, s, value):
@@ -288,38 +368,35 @@
 def summed(keep, send):
     both = ("gz", "gy")
     nz, ny = lax.axis_size("gz"), lax.axis_size("gy")
-    z, y = lax.axis_index("gz"), lax.axis_index("gy")
-    core, up, along = y % 2, (y // 2) % 2, z % 2
-    first = jnp.where(core == 0, along, up)
-    second = jnp.where(core == 0, up, along)
-
     to_core = partners(nz, ny, lambda z, y: (z, y ^ 1))
     to_first = partners(nz, ny, lambda z, y: (z ^ 1, y) if y % 2 == 0 else (z, y ^ 2))
     to_second = partners(nz, ny, lambda z, y: (z, y ^ 2) if y % 2 == 0 else (z ^ 1, y))
 
-    def half(x, bit):
-        n = x.shape[0] // 2
-        return lax.dynamic_slice_in_dim(x, bit * n, n, 0)
-
-    got = lax.ppermute(send, both, to_core)
-    for route, bit in ((to_first, first), (to_second, second)):
-        send = half(keep, 1 - bit) + half(got, 1 - bit)
-        keep = half(keep, bit) + half(got, bit)
-        got = lax.ppermute(send, both, route)
+    def hop(x, route):
+        return lax.ppermute(x, both, route)
+
+    got = hop(send, to_core)
+    for route in (to_first, to_second):
+        n = keep.shape[0] // 2
+        send = keep[n:] + got[n:]
+        keep, mine = keep[:n], got[:n]
+        got = hop(send, route)
+        keep = keep + mine
     total = keep + got
     step = 2
     while step < nz:
-        total = total + lax.ppermute(total, both, partners(nz, ny, lambda z, y: (z ^ step, y)))
+        far = partners(nz, ny, lambda z, y: (z ^ step, y))
+        total = total + hop(total, far)
         step *= 2
 
     a = total.astype(BF16)
-    b = lax.ppermute(a, both, to_second)
+    b = hop(a, to_second)
     ab = jnp.concatenate([a, b], 0)
-    c = lax.ppermute(ab, both, to_first)
-    d = lax.ppermute(jnp.concatenate([ab, c], 0), both, to_core)
+    c = hop(ab, to_first)
+    d = hop(jnp.concatenate([ab, c], 0), to_core)
     vmem = pl.BlockSpec(memory_space=pltpu.VMEM)
     return pl.pallas_call(
-        functools.partial(join_kernel, nz=nz, ny=ny),
+        join_kernel,
         in_specs=[vmem] * 4,
         out_specs=vmem,
         out_shape=jax.ShapeDtypeStruct((8 * a.shape[0], a.shape[1]), F32),
@@ -336,16 +413,17 @@
     zo, yo = zi // 2, yi // 2
     taps = kernel.reshape((27,) + kernel.shape[3:])
     split = features.reshape(zo, 2, yo, 2, pairs, chans)
-    mask = jnp.repeat(occupancy[0, 0], pairs // occupancy.shape[2]).astype(BF16)[None, :, None]
-
-    gz = shifted(upstream[0] * mask, "gz", -1)
-    gy = shifted(jnp.concatenate([upstream[:, 0] * mask, gz[:1]], 0), "gy", -1)
-    keep, send = weight_grad(occupancy, split, upstream, gz, gy, chans // 2)
+    gz, gy, rz, ry = rims_of(occupancy, features, upstream)
+
+    gy = shifted(gy, "gy", -1)
+    gz = shifted(jnp.concatenate([gz, gy[:1]], 0), "gz", -1)
+    acc = weight_grad(occupancy, split, upstream, chans // 2)
+    keep, send = with_edges(acc, rz, ry, gz, gy)
     kernel_grad = summed(keep, send).reshape(kernel.shape)
 
-    fz = shifted(features[-1] * mask, "gz", 1)
-    fy = shifted(jnp.concatenate([fz[-1:], features[:, -1] * mask], 0), "gy", 1)
-    coarse = coarse_conv(occupancy, taps, split, fz.reshape(yo, 2, pairs, chans), fy)
+    fy = shifted(ry, "gy", 1)
+    fz = shifted(jnp.concatenate([fy[-1:], rz], 0), "gz", 1)
+    coarse = coarse_conv(occupancy, taps, split, fz, fy)
     feature_grad = data_grad(occupancy, taps, upstream, gz, gy).reshape(features.shape)
     return (coarse, feature_grad, kernel_grad)
 

time: 71.4 us -> 59.2 us (0.83)
  waiting for transfers between devices: 27.2 us -> 20.9 us
  other arithmetic: 6.14 us -> 0.17 us
  local copies, waits for them, and re-layouts: 3.47 us -> 0.02 us
  starting transfers between devices: 20.1 us -> 21.9 us
  Pallas kernels: 13.3 us -> 14.8 us
    ppermute x4, waiting for transfers between devices: 9.88 us -> 4.66 us  [shifted(): lax.ppermute(block, axis, [(i, i + distance) for i in range(n) if 0 <= i...]
    ppermute x8, starting transfers between devices: 12.1 us -> 16.1 us  [hop(): return lax.ppermute(x, both, route)]
    add x3, other arithmetic: 3.41 us -> 0.09 us  [the longest x1 0.06 us: summed(): keep = keep + mine]
    unnamed x14 -> x8, local copies, waits for them, and re-layouts: 3.3 us -> 0.02 us
    ppermute x4, starting transfers between devices: 8.02 us -> 5.8 us  [shifted(): lax.ppermute(block, axis, [(i, i + distance) for i in range(n) if 0 <= i...]
    pallas_call x1 -> x3, Pallas kernels: 0.99 us -> 2.58 us  [the longest x1 1.21 us: rims_of(): pl.pallas_call(body, grid=(1,), in_specs=[SCALARS, pl.BlockSpec((1, yi, p...]
    ppermute x8, waiting for transfers between devices: 17.3 us -> 16.3 us  [hop(): return lax.ppermute(x, both, route)]
    mul x2 -> x0, other arithmetic: 1.08 us -> none  [the longest x1 1 us: shards(): gy = shifted(jnp.concatenate([upstream[:, 0] * mask, gz[:1]], 0), 'gy', -1)]
  transfers between devices with their start and end apart: 12 -> 12, of which waited for: 9 -> 9; matrix products, arithmetic and copies ran while one was open for 0% -> 0% of each run, Pallas kernels for 13% -> 21%
where the time goes in v1:
time: 59.2 us; the launch traced here: 58.6 us
  starting transfers between devices  21.9 us (37%)
  waiting for transfers between devices  20.9 us (35%)
  Pallas kernels  14.8 us (25%)
  between operations  0.79 us (1%)
    ppermute x8, waiting for transfers between devices, hop(): return lax.ppermute(x, both, route)  16.3 us
    ppermute x8, starting transfers between devices, hop(): return lax.ppermute(x, both, route)  16.1 us
    ppermute x4, starting transfers between devices, shifted(): lax.ppermute(block, axis, [(i, i + distance) for i in range(n) if 0 <= i...  5.8 us
    pallas_call x1, Pallas kernels, data_grad(): pl.pallas_call(data_kernel, grid=(zo // na,), in_specs=[SCALARS, whole(ke...  5.6 us
    ppermute x4, waiting for transfers between devices, shifted(): lax.ppermute(block, axis, [(i, i + distance) for i in range(n) if 0 <= i...  4.66 us
    pallas_call x1, Pallas kernels, coarse_conv(): pl.pallas_call(coarse_kernel, grid=(zo // na,), in_specs=[SCALARS, whole(...  3.58 us
    pallas_call x1, Pallas kernels, weight_grad(): pl.pallas_call(weight_kernel, grid=(zo // na,), in_specs=[SCALARS, leadin...  3.06 us
    pallas_call x1, Pallas kernels, rims_of(): pl.pallas_call(body, grid=(1,), in_specs=[SCALARS, pl.BlockSpec((1, yi, p...  1.21 us
  transfers between devices with their start and end apart: 12, of which 9 were waited for; matrix products, arithmetic and copies ran while one was open for 0% of the time, Pallas kernels for 21%

profile of v1, /device:TPU:0, one launch (start us, length us, event | category | flops | bytes accessed | tf_op | source)
XLA Modules:
  0.0 58.6 jit_solution(18273404309351641155)
XLA Ops:
  0.7 1.2 %shard_map.67 = (bf16[8,32,128]{2,1,0:T(8,128)(2,1)S(1)}, bf16[8,32,128]{2,1,0:T(8,128)(2,1)S(1)}, bf16[16,32,128]{2,1,0:T(8,128)(2,1)S(1)}, bf16[16,32,128]{2,1,0:T(8,128)(2,1)S(1)}) custom-call(s32[1,1,4]{2,1,0:T(1,128)} %occ_ref.7, bf16[16,16,32,128]{3,2,1,0:T(8,128)(2,1)} %fb_ref.1, bf16[16,16,32,128]{3,2,1,0:T(8,128)(2,1)} %fb_ref.1, ...), custom_call_target="tpu_custom_call" | custom-call | bytes 786432 | tf_op jit(solution)/shard_map/pallas_call | solution.py:70
  1.9 1.3 %collective-permute-start.2 = (bf16[8,32,128]{2,1,0:T(8,128)(2,1)S(1)}, bf16[8,32,128]{2,1,0:T(8,128)(2,1)S(1)}, u32[]{:S(2)}, u32[]{:S(2)}) collective-permute-start(bf16[8,32,128]{2,1,0:T(8,128)(2,1)S(1)} %get-tuple-element.12), channel_id=1, source_target_pairs={{1,0},{2,1},{3,2},{5,4},{6,5},{7,6},{9,8},{10,9},{11,10},{13,12},{... | collective-permute-start | bytes 196616 | tf_op jit(solution)/shard_map/ppermute | solution.py:338
  3.2 1.8 %collective-permute-done.2.gy_ref = bf16[8,32,128]{2,1,0:T(8,128)(2,1)S(1)} collective-permute-done((bf16[8,32,128]{2,1,0:T(8,128)(2,1)S(1)}, bf16[8,32,128]{2,1,0:T(8,128)(2,1)S(1)}, u32[]{:S(2)}, u32[]{:S(2)}) %collective-permute-start.2) | collective-permute-done | bytes 65568 | tf_op jit(solution)/shard_map/ppermute | solution.py:338
  5.0 1.3 %collective-permute-start.3 = (bf16[9,32,128]{2,1,0:T(8,128)(2,1)S(1)}, bf16[9,32,128]{2,1,0:T(8,128)(2,1)S(1)}, u32[]{:S(2)}, u32[]{:S(2)}) collective-permute-start(bf16[9,32,128]{2,1,0:T(8,128)(2,1)S(1)} %pad_maximum_fusion.3), channel_id=1, source_target_pairs={{4,0},{8,4},{12,8},{16,12},{20,16},{24,20},{28,24},{5,1},{9,5},{13... | collective-permute-start | bytes 221192 | tf_op jit(solution)/shard_map/ppermute | solution.py:338
  6.4 3.1 %shard_map.70.acc_ref = f32[1152,256]{1,0:T(8,128)S(1)} custom-call(s32[1,1,4]{2,1,0:T(1,128)S(1)} %copy-done.2, bf16[8,2,8,2,32,128]{5,4,3,2,1,0:T(8,128)(2,1)S(1)} %bitcast.4, bf16[8,8,32,128]{3,2,1,0:T(8,128)(2,1)S(1)} %copy-done.1), custom_call_target="tpu_custom_call" | custom-call | flops 1207959552 | bytes 2097152 | tf_op jit(solution)/shard_map/pallas_call | solution.py:268
  9.4 2.8 %collective-permute-done.3.gz_ref = bf16[9,32,128]{2,1,0:T(8,128)(2,1)S(1)} collective-permute-done((bf16[9,32,128]{2,1,0:T(8,128)(2,1)S(1)}, bf16[9,32,128]{2,1,0:T(8,128)(2,1)S(1)}, u32[]{:S(2)}, u32[]{:S(2)}) %collective-permute-start.3) | collective-permute-done | bytes 73760 | tf_op jit(solution)/shard_map/ppermute | solution.py:338
  12.2 0.4 shard_map.71
  12.6 0.0 copy-start.3
  12.6 1.8 %collective-permute-start.4 = (f32[864,128]{1,0:T(8,128)S(1)}, f32[864,128]{1,0:T(8,128)S(1)}, u32[]{:S(2)}, u32[]{:S(2)}) collective-permute-start(f32[864,128]{1,0:T(8,128)S(1)} %get-tuple-element.14), channel_id=1, source_target_pairs={{0,1},{1,0},{2,3},{3,2},{4,5},{5,4},{6,7},{7,6},{8,9},{9,8},{10,11... | collective-permute-start | bytes 1327112 | tf_op jit(solution)/shard_map/ppermute | solution.py:376
  14.4 1.4 %collective-permute-done.4 = f32[864,128]{1,0:T(8,128)S(1)} collective-permute-done((f32[864,128]{1,0:T(8,128)S(1)}, f32[864,128]{1,0:T(8,128)S(1)}, u32[]{:S(2)}, u32[]{:S(2)}) %collective-permute-start.4) | collective-permute-done | bytes 442400 | tf_op jit(solution)/shard_map/ppermute | solution.py:376
  15.8 0.1 slice_add_fusion.1
  15.9 2.5 %collective-permute-start.5 = (f32[432,128]{1,0:T(8,128)S(1)}, f32[432,128]{1,0:T(8,128)S(1)}, u32[]{:S(2)}, u32[]{:S(2)}) collective-permute-start(f32[432,128]{1,0:T(8,128)S(1)} %get-tuple-element.16), channel_id=1, source_target_pairs={{0,4},{1,3},{2,6},{3,1},{4,0},{5,7},{6,2},{7,5},{8,12},{9,11},{10,... | collective-permute-start | bytes 663560 | tf_op jit(solution)/shard_map/ppermute | solution.py:376
  18.3 3.9 %collective-permute-done.5 = f32[432,128]{1,0:T(8,128)S(1)} collective-permute-done((f32[432,128]{1,0:T(8,128)S(1)}, f32[432,128]{1,0:T(8,128)S(1)}, u32[]{:S(2)}, u32[]{:S(2)}) %collective-permute-start.5) | collective-permute-done | bytes 221216 | tf_op jit(solution)/shard_map/ppermute | solution.py:376
  22.3 1.4 %collective-permute-start.6 = (f32[216,128]{1,0:T(8,128)S(1)}, f32[216,128]{1,0:T(8,128)S(1)}, u32[]{:S(2)}, u32[]{:S(2)}) collective-permute-start(f32[216,128]{1,0:T(8,128)S(1)} %slice_add_fusion.2), channel_id=1, source_target_pairs={{0,2},{1,5},{2,0},{3,7},{4,6},{5,1},{6,4},{7,3},{8,10},{9,13},{10,... | collective-permute-start | bytes 331784 | tf_op jit(solution)/shard_map/ppermute | solution.py:376
  23.7 3.4 %collective-permute-done.6 = f32[216,128]{1,0:T(8,128)S(1)} collective-permute-done((f32[216,128]{1,0:T(8,128)S(1)}, f32[216,128]{1,0:T(8,128)S(1)}, u32[]{:S(2)}, u32[]{:S(2)}) %collective-permute-start.6) | collective-permute-done | bytes 110624 | tf_op jit(solution)/shard_map/ppermute | solution.py:376
  27.1 2.3 %collective-permute-start.7 = (f32[216,128]{1,0:T(8,128)S(1)}, f32[216,128]{1,0:T(8,128)S(1)}, u32[]{:S(2)}, u32[]{:S(2)}) collective-permute-start(f32[216,128]{1,0:T(8,128)S(1)} %fusion), channel_id=1, source_target_pairs={{0,8},{1,9},{2,10},{3,11},{4,12},{5,13},{6,14},{7,15},{8,0},{9,1},... | collective-permute-start | bytes 331784 | tf_op jit(solution)/shard_map/ppermute | solution.py:376
  29.4 2.7 %collective-permute-done.7 = f32[216,128]{1,0:T(8,128)S(1)} collective-permute-done((f32[216,128]{1,0:T(8,128)S(1)}, f32[216,128]{1,0:T(8,128)S(1)}, u32[]{:S(2)}, u32[]{:S(2)}) %collective-permute-start.7) | collective-permute-done | bytes 110624 | tf_op jit(solution)/shard_map/ppermute | solution.py:376
  32.2 3.3 %collective-permute-start.8 = (f32[216,128]{1,0:T(8,128)S(1)}, f32[216,128]{1,0:T(8,128)S(1)}, u32[]{:S(2)}, u32[]{:S(2)}) collective-permute-start(f32[216,128]{1,0:T(8,128)S(1)} %add.26), channel_id=1, source_target_pairs={{0,16},{1,17},{2,18},{3,19},{4,20},{5,21},{6,22},{7,23},{8,24},{9,... | collective-permute-start | bytes 331784 | tf_op jit(solution)/shard_map/ppermute | solution.py:376
  35.5 1.3 %collective-permute-start = (bf16[16,32,128]{2,1,0:T(8,128)(2,1)S(1)}, bf16[16,32,128]{2,1,0:T(8,128)(2,1)S(1)}, u32[]{:S(2)}, u32[]{:S(2)}) collective-permute-start(bf16[16,32,128]{2,1,0:T(8,128)(2,1)S(1)} %get-tuple-element.9.fy_ref), channel_id=1, source_target_pairs={{0,1},{1,2},{2,3},{4,5},{5,6},{6,7},{8,9},{9,10},{10,11},{12,13},{... | collective-permute-start | bytes 393224 | tf_op jit(solution)/shard_map/ppermute | solution.py:338
  36.8 1.4 %collective-permute-done.8 = f32[216,128]{1,0:T(8,128)S(1)} collective-permute-done((f32[216,128]{1,0:T(8,128)S(1)}, f32[216,128]{1,0:T(8,128)S(1)}, u32[]{:S(2)}, u32[]{:S(2)}) %collective-permute-start.8) | collective-permute-done | bytes 110624 | tf_op jit(solution)/shard_map/ppermute | solution.py:376
  38.2 2.1 %collective-permute-start.9 = (bf16[216,128]{1,0:T(8,128)(2,1)S(1)}, bf16[216,128]{1,0:T(8,128)(2,1)S(1)}, u32[]{:S(2)}, u32[]{:S(2)}) collective-permute-start(bf16[216,128]{1,0:T(8,128)(2,1)S(1)} %add_convert_fusion.a_ref), channel_id=1, source_target_pairs={{0,2},{1,5},{2,0},{3,7},{4,6},{5,1},{6,4},{7,3},{8,10},{9,13},{10,... | collective-permute-start | bytes 165896 | tf_op jit(solution)/shard_map/ppermute | solution.py:376
  40.3 0.0 collective-permute-done.fy_ref
  40.3 2.1 %collective-permute-done.9.b_ref = bf16[216,128]{1,0:T(8,128)(2,1)S(1)} collective-permute-done((bf16[216,128]{1,0:T(8,128)(2,1)S(1)}, bf16[216,128]{1,0:T(8,128)(2,1)S(1)}, u32[]{:S(2)}, u32[]{:S(2)}) %collective-permute-start.9) | collective-permute-done | bytes 55328 | tf_op jit(solution)/shard_map/ppermute | solution.py:376
  42.5 2.7 %collective-permute-start.10 = (bf16[432,128]{1,0:T(8,128)(2,1)S(1)}, bf16[432,128]{1,0:T(8,128)(2,1)S(1)}, u32[]{:S(2)}, u32[]{:S(2)}) collective-permute-start(bf16[432,128]{1,0:T(8,128)(2,1)S(1)} %pad_maximum_fusion.2), channel_id=1, source_target_pairs={{0,4},{1,3},{2,6},{3,1},{4,0},{5,7},{6,2},{7,5},{8,12},{9,11},{10,... | collective-permute-start | bytes 331784 | tf_op jit(solution)/shard_map/ppermute | solution.py:376
  45.2 1.9 %collective-permute-start.1 = (bf16[17,32,128]{2,1,0:T(8,128)(2,1)S(1)}, bf16[17,32,128]{2,1,0:T(8,128)(2,1)S(1)}, u32[]{:S(2)}, u32[]{:S(2)}) collective-permute-start(bf16[17,32,128]{2,1,0:T(8,128)(2,1)S(1)} %pad_maximum_fusion.1), channel_id=1, source_target_pairs={{0,4},{4,8},{8,12},{12,16},{16,20},{20,24},{24,28},{1,5},{5,9},{9,... | collective-permute-start | bytes 417800 | tf_op jit(solution)/shard_map/ppermute | solution.py:338
  47.1 1.2 %collective-permute-done.10.c_ref = bf16[432,128]{1,0:T(8,128)(2,1)S(1)} collective-permute-done((bf16[432,128]{1,0:T(8,128)(2,1)S(1)}, bf16[432,128]{1,0:T(8,128)(2,1)S(1)}, u32[]{:S(2)}, u32[]{:S(2)}) %collective-permute-start.10) | collective-permute-done | bytes 110624 | tf_op jit(solution)/shard_map/ppermute | solution.py:376
  48.4 0.1 collective-permute-start.11
  48.5 5.6 %shard_map.69 = bf16[8,2,8,2,32,128]{5,4,3,2,1,0:T(8,128)(2,1)} custom-call(s32[1,1,4]{2,1,0:T(1,128)S(1)} %copy-done.2, bf16[27,64,128]{2,1,0:T(8,128)(2,1)S(1)} %bitcast.6, bf16[8,8,32,128]{3,2,1,0:T(8,128)(2,1)S(1)} %copy-done.1, bf16[9,32,128]{2,1,0:T(8,128)(2,1)S(1)} %collective-permute-done.3.gz_ref, bf16[8,32,128]{2,1,0:T(8,128)(2,1)S(1)} %collective-permute-done.2.gy_ref), custom_call_target="tpu_custom_call" | custom-call | flops 1207959552 | bytes 2097152 | tf_op jit(solution)/shard_map/pallas_call | solution.py:301
  54.1 0.0 collective-permute-done.1.fz_ref
  54.1 3.6 %shard_map.68 = bf16[8,8,32,128]{3,2,1,0:T(8,128)(2,1)} custom-call(s32[1,1,4]{2,1,0:T(1,128)S(1)} %copy-done.2, bf16[27,64,128]{2,1,0:T(8,128)(2,1)S(1)} %bitcast.7, bf16[8,2,8,2,32,128]{5,4,3,2,1,0:T(8,128)(2,1)S(1)} %bitcast.5, bf16[17,32,128]{2,1,0:T(8,128)(2,1)S(1)} %collective-permute-done.1.fz_ref, bf16[16,32,128]{2,1,0:T(8,128)(2,1)S(1)} %collective-permute-done.fy_ref), custom_call_target="tpu_custom_call" | custom-call | flops 1207959552 | bytes 2097152 | tf_op jit(solution)/shard_map/pallas_call | solution.py:320
  57.6 0.0 collective-permute-done.11.d_ref
  57.6 1.0 %shard_map.72 = f32[1728,128]{1,0:T(8,128)} custom-call(bf16[216,128]{1,0:T(8,128)(2,1)S(1)} %add_convert_fusion.a_ref, bf16[216,128]{1,0:T(8,128)(2,1)S(1)} %collective-permute-done.9.b_ref, bf16[432,128]{1,0:T(8,128)(2,1)S(1)} %collective-permute-done.10.c_ref, bf16[864,128]{1,0:T(8,128)(2,1)S(1)} %collective-permute-done.11.d_ref), custom_call_target="tpu_custom_call" | custom-call | bytes 1327104 | tf_op jit(solution)/shard_map/pallas_call | solution.py:398
  (17 shorter events, 0.1 us)
Async XLA Ops:
  0.6 5.7 %copy-start.2 = (s32[1,1,4]{2,1,0:T(1,128)S(1)}, s32[1,1,4]{2,1,0:T(1,128)}, u32[]{:S(2)}) copy-start(s32[1,1,4]{2,1,0:T(1,128)} %occ_ref.7) | copy-start | bytes 52
  0.6 5.7 %copy-start.1 = (bf16[8,8,32,128]{3,2,1,0:T(8,128)(2,1)S(1)}, bf16[8,8,32,128]{3,2,1,0:T(8,128)(2,1)}, u32[]{:S(2)}) copy-start(bf16[8,8,32,128]{3,2,1,0:T(8,128)(2,1)} %g_ref.3) | copy-start | bytes 1572868
  0.7 5.7 %copy-start = (bf16[16,16,32,128]{3,2,1,0:T(8,128)(2,1)S(1)}, bf16[16,16,32,128]{3,2,1,0:T(8,128)(2,1)}, u32[]{:S(2)}) copy-start(bf16[16,16,32,128]{3,2,1,0:T(8,128)(2,1)} %fb_ref.1) | copy-start | bytes 6291460
  1.9 3.1 %collective-permute-start.2 = (bf16[8,32,128]{2,1,0:T(8,128)(2,1)S(1)}, bf16[8,32,128]{2,1,0:T(8,128)(2,1)S(1)}, u32[]{:S(2)}, u32[]{:S(2)}) collective-permute-start(bf16[8,32,128]{2,1,0:T(8,128)(2,1)S(1)} %get-tuple-element.12), channel_id=1, source_target_pairs={{1,0},{2,1},{3,2},{5,4},{6,5},{7,6},{9,8},{10,9},{11,10},{13,12},{... | collective-permute-start | bytes 196616 | tf_op jit(solution)/shard_map/ppermute | solution.py:338
  5.0 7.2 %collective-permute-start.3 = (bf16[9,32,128]{2,1,0:T(8,128)(2,1)S(1)}, bf16[9,32,128]{2,1,0:T(8,128)(2,1)S(1)}, u32[]{:S(2)}, u32[]{:S(2)}) collective-permute-start(bf16[9,32,128]{2,1,0:T(8,128)(2,1)S(1)} %pad_maximum_fusion.3), channel_id=1, source_target_pairs={{4,0},{8,4},{12,8},{16,12},{20,16},{24,20},{28,24},{5,1},{9,5},{13... | collective-permute-start | bytes 221192 | tf_op jit(solution)/shard_map/ppermute | solution.py:338
  12.6 35.8 %copy-start.3 = (bf16[3,3,3,64,128]{4,3,2,1,0:T(8,128)(2,1)S(1)}, bf16[3,3,3,64,128]{4,3,2,1,0:T(8,128)(2,1)}, u32[]{:S(2)}) copy-start(bf16[3,3,3,64,128]{4,3,2,1,0:T(8,128)(2,1)} %param.6) | copy-start | bytes 1327108
  12.6 3.2 %collective-permute-start.4 = (f32[864,128]{1,0:T(8,128)S(1)}, f32[864,128]{1,0:T(8,128)S(1)}, u32[]{:S(2)}, u32[]{:S(2)}) collective-permute-start(f32[864,128]{1,0:T(8,128)S(1)} %get-tuple-element.14), channel_id=1, source_target_pairs={{0,1},{1,0},{2,3},{3,2},{4,5},{5,4},{6,7},{7,6},{8,9},{9,8},{10,11... | collective-permute-start | bytes 1327112 | tf_op jit(solution)/shard_map/ppermute | solution.py:376
  15.9 6.4 %collective-permute-start.5 = (f32[432,128]{1,0:T(8,128)S(1)}, f32[432,128]{1,0:T(8,128)S(1)}, u32[]{:S(2)}, u32[]{:S(2)}) collective-permute-start(f32[432,128]{1,0:T(8,128)S(1)} %get-tuple-element.16), channel_id=1, source_target_pairs={{0,4},{1,3},{2,6},{3,1},{4,0},{5,7},{6,2},{7,5},{8,12},{9,11},{10,... | collective-permute-start | bytes 663560 | tf_op jit(solution)/shard_map/ppermute | solution.py:376
  22.3 4.8 %collective-permute-start.6 = (f32[216,128]{1,0:T(8,128)S(1)}, f32[216,128]{1,0:T(8,128)S(1)}, u32[]{:S(2)}, u32[]{:S(2)}) collective-permute-start(f32[216,128]{1,0:T(8,128)S(1)} %slice_add_fusion.2), channel_id=1, source_target_pairs={{0,2},{1,5},{2,0},{3,7},{4,6},{5,1},{6,4},{7,3},{8,10},{9,13},{10,... | collective-permute-start | bytes 331784 | tf_op jit(solution)/shard_map/ppermute | solution.py:376
  27.1 5.0 %collective-permute-start.7 = (f32[216,128]{1,0:T(8,128)S(1)}, f32[216,128]{1,0:T(8,128)S(1)}, u32[]{:S(2)}, u32[]{:S(2)}) collective-permute-start(f32[216,128]{1,0:T(8,128)S(1)} %fusion), channel_id=1, source_target_pairs={{0,8},{1,9},{2,10},{3,11},{4,12},{5,13},{6,14},{7,15},{8,0},{9,1},... | collective-permute-start | bytes 331784 | tf_op jit(solution)/shard_map/ppermute | solution.py:376
  32.2 6.1 %collective-permute-start.8 = (f32[216,128]{1,0:T(8,128)S(1)}, f32[216,128]{1,0:T(8,128)S(1)}, u32[]{:S(2)}, u32[]{:S(2)}) collective-permute-start(f32[216,128]{1,0:T(8,128)S(1)} %add.26), channel_id=1, source_target_pairs={{0,16},{1,17},{2,18},{3,19},{4,20},{5,21},{6,22},{7,23},{8,24},{9,... | collective-permute-start | bytes 331784 | tf_op jit(solution)/shard_map/ppermute | solution.py:376
  35.5 4.8 %collective-permute-start = (bf16[16,32,128]{2,1,0:T(8,128)(2,1)S(1)}, bf16[16,32,128]{2,1,0:T(8,128)(2,1)S(1)}, u32[]{:S(2)}, u32[]{:S(2)}) collective-permute-start(bf16[16,32,128]{2,1,0:T(8,128)(2,1)S(1)} %get-tuple-element.9.fy_ref), channel_id=1, source_target_pairs={{0,1},{1,2},{2,3},{4,5},{5,6},{6,7},{8,9},{9,10},{10,11},{12,13},{... | collective-permute-start | bytes 393224 | tf_op jit(solution)/shard_map/ppermute | solution.py:338
  38.2 4.2 %collective-permute-start.9 = (bf16[216,128]{1,0:T(8,128)(2,1)S(1)}, bf16[216,128]{1,0:T(8,128)(2,1)S(1)}, u32[]{:S(2)}, u32[]{:S(2)}) collective-permute-start(bf16[216,128]{1,0:T(8,128)(2,1)S(1)} %add_convert_fusion.a_ref), channel_id=1, source_target_pairs={{0,2},{1,5},{2,0},{3,7},{4,6},{5,1},{6,4},{7,3},{8,10},{9,13},{10,... | collective-permute-start | bytes 165896 | tf_op jit(solution)/shard_map/ppermute | solution.py:376
  42.5 5.9 %collective-permute-start.10 = (bf16[432,128]{1,0:T(8,128)(2,1)S(1)}, bf16[432,128]{1,0:T(8,128)(2,1)S(1)}, u32[]{:S(2)}, u32[]{:S(2)}) collective-permute-start(bf16[432,128]{1,0:T(8,128)(2,1)S(1)} %pad_maximum_fusion.2), channel_id=1, source_target_pairs={{0,4},{1,3},{2,6},{3,1},{4,0},{5,7},{6,2},{7,5},{8,12},{9,11},{10,... | collective-permute-start | bytes 331784 | tf_op jit(solution)/shard_map/ppermute | solution.py:376
  45.2 8.9 %collective-permute-start.1 = (bf16[17,32,128]{2,1,0:T(8,128)(2,1)S(1)}, bf16[17,32,128]{2,1,0:T(8,128)(2,1)S(1)}, u32[]{:S(2)}, u32[]{:S(2)}) collective-permute-start(bf16[17,32,128]{2,1,0:T(8,128)(2,1)S(1)} %pad_maximum_fusion.1), channel_id=1, source_target_pairs={{0,4},{4,8},{8,12},{12,16},{16,20},{20,24},{24,28},{1,5},{5,9},{9,... | collective-permute-start | bytes 417800 | tf_op jit(solution)/shard_map/ppermute | solution.py:338
  48.4 9.3 %collective-permute-start.11 = (bf16[864,128]{1,0:T(8,128)(2,1)S(1)}, bf16[864,128]{1,0:T(8,128)(2,1)S(1)}, u32[]{:S(2)}, u32[]{:S(2)}) collective-permute-start(bf16[864,128]{1,0:T(8,128)(2,1)S(1)} %pad_maximum_fusion), channel_id=1, source_target_pairs={{0,1},{1,0},{2,3},{3,2},{4,5},{5,4},{6,7},{7,6},{8,9},{9,8},{10,11... | collective-permute-start | bytes 663560 | tf_op jit(solution)/shard_map/ppermute | solution.py:376

commit v2 on v1

--- a/solution.py
+++ b/solution.py
@@ -1,3 +1,5 @@
+import functools
+
 import jax
 import jax.numpy as jnp
 from jax import lax
@@ -28,15 +30,6 @@
     wide = pltpu.roll(g.astype(F32), pairs - 1, axis)
     last = lax.broadcasted_iota(jnp.int32, wide.shape, axis) == pairs - 1
     return jnp.concatenate([g, jnp.where(last, 0.0, wide).astype(BF16)], -1)
-
-
-def fill_grads(gext, g_ref, gz_ref, gy_ref, occ_ref):
-    zo, yo, pairs, cout = g_ref.shape
-    mask = row_mask(occ_ref, pairs, cout).astype(BF16)
-    for a in range(zo):
-        gext[a, :yo] = with_next(g_ref[a] * mask)
-    gext[:zo, yo] = with_next(gy_ref[...])
-    gext[zo] = with_next(gz_ref[...])
 
 
 def grad_rows(gext, a0, na, da, db):
@@ -85,35 +78,28 @@
 
 
 def weight_kernel(occ_ref, f_ref, g_ref, acc_ref, gext):
-    step = pl.program_id(0)
-    na, _, yo, _, pairs, chans = f_ref.shape
-    zo, _, _, cout = g_ref.shape
-
-    @pl.when(step == 0)
-    def _():
-        mask = row_mask(occ_ref, pairs, cout).astype(BF16)
-        for a in range(zo):
-            gext[a, :yo] = with_next(g_ref[a] * mask)
-        gext[zo] = jnp.zeros(gext.shape[1:], BF16)
-        gext[:, yo] = jnp.zeros((zo + 1, pairs, 2 * cout), BF16)
-        acc_ref[...] = jnp.zeros_like(acc_ref)
-
+    zo, _, yo, _, pairs, chans = f_ref.shape
+    cout = g_ref.shape[3]
+    mask = row_mask(occ_ref, pairs, cout).astype(BF16)
+    for a in range(zo):
+        gext[a, :yo] = with_next(g_ref[a] * mask)
+    gext[zo] = jnp.zeros(gext.shape[1:], BF16)
+    gext[:, yo] = jnp.zeros((zo + 1, pairs, 2 * cout), BF16)
     mask = row_mask(occ_ref, pairs, chans).astype(BF16)
 
     def rows(pz, py):
-        return (f_ref[:, pz, :, py] * mask).reshape(na * yo * pairs, chans)
+        return (f_ref[:, pz, :, py] * mask).reshape(zo * yo * pairs, chans)
 
     ee, eo, oe, oo = rows(0, 0), rows(0, 1), rows(1, 0), rows(1, 1)
-    a0 = step * na
     c = chans
 
     def product(x, da, db):
-        return rows_product(x, grad_rows(gext, a0, na, da, db))
-
-    acc_ref[: 4 * c] += product(jnp.concatenate([ee, eo, oe, oo], 1), 0, 0)
-    acc_ref[4 * c : 6 * c] += product(jnp.concatenate([eo, oo], 1), 0, 1)
-    acc_ref[6 * c : 8 * c] += product(jnp.concatenate([oe, oo], 1), 1, 0)
-    acc_ref[8 * c : 9 * c] += product(oo, 1, 1)
+        return rows_product(x, grad_rows(gext, 0, zo, da, db))
+
+    acc_ref[: 4 * c] = product(jnp.concatenate([ee, eo, oe, oo], 1), 0, 0)
+    acc_ref[4 * c : 6 * c] = product(jnp.concatenate([eo, oo], 1), 0, 1)
+    acc_ref[6 * c : 8 * c] = product(jnp.concatenate([oe, oo], 1), 1, 0)
+    acc_ref[8 * c : 9 * c] = product(oo, 1, 1)
 
 
 def rows_product(x, g):
@@ -122,10 +108,7 @@
 
 def place():
     z, y = lax.axis_index("gz"), lax.axis_index("gy")
-    core, up, along = y % 2, (y // 2) % 2, z % 2
-    first = jnp.where(core == 0, along, up)
-    second = jnp.where(core == 0, up, along)
-    return core, first, second
+    return y % 2, 2 * (z % 2) + (y // 2) % 2
 
 
 def edge_kernel(acc_ref, fz_ref, fy_ref, gz_ref, gy_ref, keep_ref, send_ref, acc, flat):
@@ -153,32 +136,41 @@
         source = acc_ref if s < 4 else acc
         flat[t : t + cin] = source[r + cin : r + chans, cout:]
         flat[t + cin : t + 3 * cin] = source[r : r + chans, :cout]
-    core, first, second = place()
+    core, quarter = place()
     part = keep_ref.shape[0] // 4
-    for f in range(2):
-        for s in range(2):
-            to = (2 * f + s) * part
-            mine = ((core * 2 + (first ^ f)) * 2 + (second ^ s)) * part
-            keep_ref[to : to + part] = flat[pl.ds(pl.multiple_of(mine, 8), part)]
-            its = (((1 - core) * 2 + (second ^ f)) * 2 + (first ^ s)) * part
-            send_ref[to : to + part] = flat[pl.ds(pl.multiple_of(its, 8), part)]
-
-
-def data_kernel(occ_ref, k_ref, g_ref, gz_ref, gy_ref, out_ref, gext, taps):
+    for r in range(4):
+        rows = slice(r * part, (r + 1) * part)
+        mine = (core * 4 + (quarter ^ r)) * part
+        keep_ref[rows] = flat[pl.ds(pl.multiple_of(mine, 8), part)]
+        its = ((1 - core) * 4 + (quarter ^ r)) * part
+        send_ref[rows] = flat[pl.ds(pl.multiple_of(its, 8), part)]
+
+
+def data_kernel(occ_ref, k_ref, g_ref, gz_ref, gy_ref, *rest, first):
+    out_ref, gext, taps = rest[-3:]
     step = pl.program_id(0)
     na, _, yo, _, pairs, chans = out_ref.shape
+    zo = g_ref.shape[0]
+    count = gext.shape[0] - 1
 
     @pl.when(step == 0)
     def _():
-        fill_grads(gext, g_ref, gz_ref, gy_ref, occ_ref)
+        mask = row_mask(occ_ref, pairs, g_ref.shape[3]).astype(BF16)
+        for a in range(count + 1):
+            if first + a < zo:
+                gext[a, :yo] = with_next(g_ref[first + a] * mask)
+        near = min(count + 1, zo - first)
+        gext[:near, yo] = with_next(gy_ref[first : first + near])
+        if near == count:
+            gext[count] = with_next(gz_ref[...])
         fill_taps(taps, k_ref)
 
     a0 = step * na
     c = chans
 
-    def product(da, db, first, count):
+    def product(da, db, at, n):
         g = grad_rows(gext, a0, na, da, db)
-        w = taps[first * c : (first + count) * c]
+        w = taps[at * c : (at + n) * c]
         return lax.dot_general(g, w, (((1,), (1,)), ((), ())), preferred_element_type=F32)
 
     mask = row_mask(occ_ref, pairs, chans)
@@ -196,7 +188,8 @@
     put(1, 1, (p00[:, 3 * c :] + p01[:, c:]) + (p10[:, c:] + p11))
 
 
-def coarse_kernel(occ_ref, k_ref, f_ref, fz_ref, fy_ref, out_ref, prev, rim, taps):
+def coarse_kernel(occ_ref, k_ref, f_ref, before_ref, fy_ref, *rest, first):
+    out_ref, prev, rim, taps = rest[-4:]
     step = pl.program_id(0)
     na, _, yo, _, pairs, chans = f_ref.shape
     cout = out_ref.shape[3]
@@ -204,9 +197,13 @@
     @pl.when(step == 0)
     def _():
         fill_taps(taps, k_ref)
-        prev[...] = fz_ref[1:].reshape(prev.shape)
-        rim[0] = fz_ref[0]
-        rim[1:] = fy_ref[...]
+        if first == 0:
+            prev[...] = before_ref[1:].reshape(prev.shape)
+            rim[0] = before_ref[0]
+            rim[1:] = fy_ref[: rim.shape[0] - 1]
+        else:
+            prev[...] = before_ref[0, 1] * row_mask(occ_ref, pairs, chans).astype(BF16)
+            rim[...] = fy_ref[2 * first - 1 : 2 * first - 1 + rim.shape[0]]
 
     mask = row_mask(occ_ref, pairs, chans).astype(BF16)
     even = f_ref[:, 0] * mask
@@ -248,11 +245,6 @@
     return pl.BlockSpec(shape, lambda i: (0,) * len(shape))
 
 
-def leading(shape, n):
-    block = (n,) + tuple(shape[1:])
-    return pl.BlockSpec(block, lambda i: (i,) + (0,) * (len(shape) - 1))
-
-
 SCALARS = pl.BlockSpec(memory_space=pltpu.SMEM)
 PARAMS = pltpu.CompilerParams(dimension_semantics=("arbitrary",), vmem_limit_bytes=16 << 20)
 
@@ -261,18 +253,18 @@
     return pl.CostEstimate(flops=int(flops), bytes_accessed=int(nbytes), transcendentals=0)
 
 
-def weight_grad(occ, split, grad, cin, na=2):
+def weight_grad(occ, split, grad, cin):
     zo, yo, pairs, cout = grad.shape
     chans = 2 * cin
     shape = (9 * chans, 2 * cout)
+    vmem = pl.BlockSpec(memory_space=pltpu.VMEM)
     return pl.pallas_call(
         weight_kernel,
-        grid=(zo // na,),
-        in_specs=[SCALARS, leading(split.shape, na), whole(grad.shape)],
-        out_specs=whole(shape),
+        in_specs=[SCALARS, vmem, vmem],
+        out_specs=vmem,
         out_shape=jax.ShapeDtypeStruct(shape, F32),
         scratch_shapes=[pltpu.VMEM((zo + 1, yo + 1, pairs, 2 * cout), BF16)],
-        compiler_params=PARAMS,
+        compiler_params=pltpu.CompilerParams(vmem_limit_bytes=16 << 20),
         cost_estimate=cost(2 * zo * yo * pairs * 9 * chans * 2 * cout, 2 * split.size),
     )(occ, split, grad)
 
@@ -293,44 +285,61 @@
     )(acc, fz, fy, gz, gy)
 
 
-def data_grad(occ, kernel, grad, gz, gy, na=1):
+def data_grad(occ, kernel, grad, gz, gy, first, count, into=None, na=2):
     zo, yo, pairs, cout = grad.shape
     cin = kernel.shape[1]
     chans = 2 * cin
     shape = (zo, 2, yo, 2, pairs, chans)
-    return pl.pallas_call(
-        data_kernel,
-        grid=(zo // na,),
-        in_specs=[SCALARS, whole(kernel.shape), whole(grad.shape), whole(gz.shape), whole(gy.shape)],
-        out_specs=leading(shape, na),
+    block = pl.BlockSpec((na,) + shape[1:], lambda i: (i + first // na, 0, 0, 0, 0, 0))
+    given = () if into is None else (into,)
+    return pl.pallas_call(
+        functools.partial(data_kernel, first=first),
+        grid=(count // na,),
+        in_specs=[SCALARS, whole(kernel.shape), whole(grad.shape), whole(gz.shape), whole(gy.shape)]
+        + [pl.BlockSpec(memory_space=pl.ANY)] * len(given),
+        out_specs=block,
         out_shape=jax.ShapeDtypeStruct(shape, BF16),
         scratch_shapes=[
-            pltpu.VMEM((zo + 1, yo + 1, pairs, 2 * cout), BF16),
+            pltpu.VMEM((count + 1, yo + 1, pairs, 2 * cout), BF16),
             pltpu.VMEM((9 * chans, 2 * cout), BF16),
         ],
+        input_output_aliases={5: 0} if given else {},
         compiler_params=PARAMS,
-        cost_estimate=cost(2 * zo * yo * pairs * 9 * chans * 2 * cout, 2 * zo * yo * pairs * 4 * chans),
-    )(occ, kernel, grad, gz, gy)
-
-
-def coarse_conv(occ, kernel, split, fz, fy, na=2):
+        cost_estimate=cost(2 * count * yo * pairs * 9 * chans * 2 * cout, 2 * count * yo * pairs * 4 * chans),
+    )(occ, kernel, grad, gz, gy, *given)
+
+
+def coarse_conv(occ, kernel, split, before, fy, first, count, into=None, na=2):
     zo, _, yo, _, pairs, chans = split.shape
     cout = kernel.shape[2]
     shape = (zo, yo, pairs, cout)
-    return pl.pallas_call(
-        coarse_kernel,
-        grid=(zo // na,),
-        in_specs=[SCALARS, whole(kernel.shape), leading(split.shape, na), whole(fz.shape), whole(fy.shape)],
-        out_specs=leading(shape, na),
+    given = () if into is None else (into,)
+    if first == 0:
+        ahead = whole(before.shape)
+    else:
+        ahead = pl.BlockSpec((1,) + split.shape[1:], lambda i: (first - 1, 0, 0, 0, 0, 0))
+    return pl.pallas_call(
+        functools.partial(coarse_kernel, first=first),
+        grid=(count // na,),
+        in_specs=[
+            SCALARS,
+            whole(kernel.shape),
+            pl.BlockSpec((na,) + split.shape[1:], lambda i: (i + first // na, 0, 0, 0, 0, 0)),
+            ahead,
+            whole(fy.shape),
+        ]
+        + [pl.BlockSpec(memory_space=pl.ANY)] * len(given),
+        out_specs=pl.BlockSpec((na,) + shape[1:], lambda i: (i + first // na, 0, 0, 0)),
         out_shape=jax.ShapeDtypeStruct(shape, BF16),
         scratch_shapes=[
             pltpu.VMEM((yo, 2, pairs, chans), BF16),
-            pltpu.VMEM((2 * zo + 1, pairs, chans), BF16),
+            pltpu.VMEM((2 * count + 1, pairs, chans), BF16),
             pltpu.VMEM((9 * chans, 2 * cout), BF16),
         ],
+        input_output_aliases={5: 0} if given else {},
         compiler_params=PARAMS,
-        cost_estimate=cost(2 * zo * yo * pairs * 9 * chans * 2 * cout, 2 * split.size),
-    )(occ, kernel, split, fz, fy)
+        cost_estimate=cost(2 * count * yo * pairs * 9 * chans * 2 * cout, 2 * split.size),
+    )(occ, kernel, split, before, fy, *given)
 
 
 def shifted(block, axis, distance):
@@ -347,62 +356,65 @@
     return moves
 
 
-def join_kernel(a_ref, b_ref, c_ref, d_ref, out_ref):
-    core, first, second = place()
-    part = a_ref.shape[0]
-
-    def put(c, f, s, value):
-        at = pl.multiple_of(((c * 2 + f) * 2 + s) * part, 8)
-        out_ref[pl.ds(at, part)] = value.astype(F32)
-
-    put(core, first, second, a_ref[...])
-    put(core, first, 1 - second, b_ref[...])
-    put(core, 1 - first, second, c_ref[:part])
-    put(core, 1 - first, 1 - second, c_ref[part:])
-    put(1 - core, second, first, d_ref[:part])
-    put(1 - core, second, 1 - first, d_ref[part : 2 * part])
-    put(1 - core, 1 - second, first, d_ref[2 * part : 3 * part])
-    put(1 - core, 1 - second, 1 - first, d_ref[3 * part :])
+def join_kernel(*refs, other):
+    out_ref, wide, sem = refs[-3:]
+    core, quarter = place()
+    half, part = wide.shape[0], wide.shape[0] // 4
+    copies = []
+    for r in range(4):
+        value = refs[0][r * part : (r + 1) * part] if other else refs[r][...]
+        wide[r * part : (r + 1) * part] = value.astype(F32)
+        at = ((core ^ 1) if other else core) * half + (quarter ^ r) * part
+        to = out_ref.at[pl.ds(pl.multiple_of(at, 8), part)]
+        copies.append(pltpu.make_async_copy(wide.at[pl.ds(r * part, part)], to, sem.at[r]))
+        copies[-1].start()
+    for copy in copies:
+        copy.wait()
+
+
+def joined(parts, other, into=None):
+    rows = sum(x.shape[0] for x in parts)
+    cols = parts[0].shape[1]
+    given = () if into is None else (into,)
+    return pl.pallas_call(
+        functools.partial(join_kernel, other=other),
+        in_specs=[pl.BlockSpec(memory_space=pltpu.VMEM)] * len(parts)
+        + [pl.BlockSpec(memory_space=pl.ANY)] * len(given),
+        out_specs=pl.BlockSpec(memory_space=pl.ANY),
+        out_shape=jax.ShapeDtypeStruct((2 * rows, cols), F32),
+        scratch_shapes=[pltpu.VMEM((rows, cols), F32), pltpu.SemaphoreType.DMA((4,))],
+        input_output_aliases={len(parts): 0} if given else {},
+        compiler_params=pltpu.CompilerParams(vmem_limit_bytes=4 << 20),
+        cost_estimate=cost(0, 6 * rows * cols),
+    )(*parts, *given)
 
 
 def summed(keep, send):
     both = ("gz", "gy")
     nz, ny = lax.axis_size("gz"), lax.axis_size("gy")
-    to_core = partners(nz, ny, lambda z, y: (z, y ^ 1))
-    to_first = partners(nz, ny, lambda z, y: (z ^ 1, y) if y % 2 == 0 else (z, y ^ 2))
-    to_second = partners(nz, ny, lambda z, y: (z, y ^ 2) if y % 2 == 0 else (z ^ 1, y))
-
-    def hop(x, route):
-        return lax.ppermute(x, both, route)
-
-    got = hop(send, to_core)
-    for route in (to_first, to_second):
-        n = keep.shape[0] // 2
-        send = keep[n:] + got[n:]
-        keep, mine = keep[:n], got[:n]
-        got = hop(send, route)
-        keep = keep + mine
-    total = keep + got
+
+    def hop(x, flip_z, flip_y):
+        return lax.ppermute(x, both, partners(nz, ny, lambda z, y: (z ^ flip_z, y ^ flip_y)))
+
+    def around(values):
+        return {r: hop(values[r], r >> 1, 2 * (r & 1)) for r in (3, 2, 1)}
+
+    got = hop(send, 0, 1)
+    n = keep.shape[0] // 4
+    sums = [keep[r * n : (r + 1) * n] + got[r * n : (r + 1) * n] for r in range(4)]
+    near = around(sums)
+    total = (sums[0] + near[3]) + (near[2] + near[1])
     step = 2
     while step < nz:
-        far = partners(nz, ny, lambda z, y: (z ^ step, y))
-        total = total + hop(total, far)
+        total = total + hop(total, step, 0)
         step *= 2
 
-    a = total.astype(BF16)
-    b = hop(a, to_second)
-    ab = jnp.concatenate([a, b], 0)
-    c = hop(ab, to_first)
-    d = hop(jnp.concatenate([ab, c], 0), to_core)
-    vmem = pl.BlockSpec(memory_space=pltpu.VMEM)
-    return pl.pallas_call(
-        join_kernel,
-        in_specs=[vmem] * 4,
-        out_specs=vmem,
-        out_shape=jax.ShapeDtypeStruct((8 * a.shape[0], a.shape[1]), F32),
-        compiler_params=pltpu.CompilerParams(vmem_limit_bytes=16 << 20),
-        cost_estimate=cost(0, 8 * a.size * 6),
-    )(a, b, c, d)
+    own = total.astype(BF16)
+    back = around([own] * 4)
+    parts = (own, back[1], back[2], back[3])
+    other = hop(jnp.concatenate(parts, 0), 0, 1)
+    out = joined(parts, False)
+    return joined((other,), True, out)
 
 
 def shards(features, occupancy, kernel, upstream):
@@ -423,8 +435,12 @@
 
     fy = shifted(ry, "gy", 1)
     fz = shifted(jnp.concatenate([fy[-1:], rz], 0), "gz", 1)
-    coarse = coarse_conv(occupancy, taps, split, fz, fy)
-    feature_grad = data_grad(occupancy, taps, upstream, gz, gy).reshape(features.shape)
+    mid = zo // 2
+    coarse = coarse_conv(occupancy, taps, split, split, fy, mid, zo - mid)
+    coarse = coarse_conv(occupancy, taps, split, fz, fy, 0, mid, coarse)
+    given = (occupancy, taps, upstream, gz, gy)
+    low = data_grad(*given, 0, mid)
+    feature_grad = data_grad(*given, mid, zo - mid, low).reshape(features.shape)
     return (coarse, feature_grad, kernel_grad)
 
 

time: 59.2 us -> 57.6 us (0.973)
  waiting for transfers between devices: 20.9 us -> 19.3 us
    ppermute x8 -> x10, waiting for transfers between devices: 16.3 us -> 13.6 us  [hop(): lax.ppermute(x, both, partners(nz, ny, lambda z, y: (z ^ flip_z, y ^ flip...]
    ppermute x8 -> x10, starting transfers between devices: 16.1 us -> 13.9 us  [hop(): lax.ppermute(x, both, partners(nz, ny, lambda z, y: (z ^ flip_z, y ^ flip...]
    ppermute x4, starting transfers between devices: 5.8 us -> 7.88 us  [shifted(): lax.ppermute(block, axis, [(i, i + distance) for i in range(n) if 0 <= i...]
    ppermute x4, waiting for transfers between devices: 4.66 us -> 5.69 us  [shifted(): lax.ppermute(block, axis, [(i, i + distance) for i in range(n) if 0 <= i...]
    pallas_call x4 -> x7, Pallas kernels: 13.2 us -> 13.8 us  [the longest x2 5.32 us: data_grad(): pl.pallas_call(functools.partial(data_kernel, first=first), grid=(count /...]
  transfers between devices with their start and end apart: 12 -> 14, of which waited for: 9 -> 8; matrix products, arithmetic and copies ran while one was open for 0% -> 0% of each run, Pallas kernels for 21% -> 23%
where the time goes in v2:
time: 57.6 us; the launch traced here: 57.4 us
  starting transfers between devices  21.8 us (38%)
  waiting for transfers between devices  19.3 us (34%)
  Pallas kernels  15.3 us (27%)
  between operations  0.83 us (1%)
    ppermute x10, starting transfers between devices, hop(): lax.ppermute(x, both, partners(nz, ny, lambda z, y: (z ^ flip_z, y ^ flip...  13.9 us
    ppermute x10, waiting for transfers between devices, hop(): lax.ppermute(x, both, partners(nz, ny, lambda z, y: (z ^ flip_z, y ^ flip...  13.6 us
    ppermute x4, starting transfers between devices, shifted(): lax.ppermute(block, axis, [(i, i + distance) for i in range(n) if 0 <= i...  7.88 us
    ppermute x4, waiting for transfers between devices, shifted(): lax.ppermute(block, axis, [(i, i + distance) for i in range(n) if 0 <= i...  5.69 us
    pallas_call x2, Pallas kernels, data_grad(): pl.pallas_call(functools.partial(data_kernel, first=first), grid=(count /...  5.32 us
    pallas_call x2, Pallas kernels, coarse_conv(): pl.pallas_call(functools.partial(coarse_kernel, first=first), grid=(count...  4.79 us
    pallas_call x1, Pallas kernels, weight_grad(): pl.pallas_call(weight_kernel, in_specs=[SCALARS, vmem, vmem], out_specs=v...  2.02 us
    pallas_call x2, Pallas kernels, joined(): pl.pallas_call(functools.partial(join_kernel, other=other), in_specs=[pl....  1.62 us
  transfers between devices with their start and end apart: 14, of which 8 were waited for; matrix products, arithmetic and copies ran while one was open for 0% of the time, Pallas kernels for 23%

profile of v2, /device:TPU:0, one launch (start us, length us, event | category | flops | bytes accessed | tf_op | source)
XLA Modules:
  0.0 57.4 jit_solution(11311101231467748877)
XLA Ops:
  0.7 1.2 %shard_map.67 = (bf16[8,32,128]{2,1,0:T(8,128)(2,1)S(1)}, bf16[8,32,128]{2,1,0:T(8,128)(2,1)S(1)}, bf16[16,32,128]{2,1,0:T(8,128)(2,1)S(1)}, bf16[16,32,128]{2,1,0:T(8,128)(2,1)S(1)}) custom-call(s32[1,1,4]{2,1,0:T(1,128)} %occ_ref.11, bf16[16,16,32,128]{3,2,1,0:T(8,128)(2,1)} %fb_ref.1, bf16[16,16,32,128]{3,2,1,0:T(8,128)(2,1)} %fb_ref.1, ...), custom_call_target="tpu_custom_call" | custom-call | bytes 786432 | tf_op jit(solution)/shard_map/pallas_call | solution.py:63
  1.9 1.3 %collective-permute-start.2 = (bf16[8,32,128]{2,1,0:T(8,128)(2,1)S(1)}, bf16[8,32,128]{2,1,0:T(8,128)(2,1)S(1)}, u32[]{:S(2)}, u32[]{:S(2)}) collective-permute-start(bf16[8,32,128]{2,1,0:T(8,128)(2,1)S(1)} %get-tuple-element.12), channel_id=1, source_target_pairs={{1,0},{2,1},{3,2},{5,4},{6,5},{7,6},{9,8},{10,9},{11,10},{13,12},{... | collective-permute-start | bytes 196616 | tf_op jit(solution)/shard_map/ppermute | solution.py:347
  3.2 1.8 %collective-permute-done.2.gy_ref = bf16[8,32,128]{2,1,0:T(8,128)(2,1)S(1)} collective-permute-done((bf16[8,32,128]{2,1,0:T(8,128)(2,1)S(1)}, bf16[8,32,128]{2,1,0:T(8,128)(2,1)S(1)}, u32[]{:S(2)}, u32[]{:S(2)}) %collective-permute-start.2) | collective-permute-done | bytes 65568 | tf_op jit(solution)/shard_map/ppermute | solution.py:347
  5.0 1.3 %collective-permute-start.3 = (bf16[9,32,128]{2,1,0:T(8,128)(2,1)S(1)}, bf16[9,32,128]{2,1,0:T(8,128)(2,1)S(1)}, u32[]{:S(2)}, u32[]{:S(2)}) collective-permute-start(bf16[9,32,128]{2,1,0:T(8,128)(2,1)S(1)} %pad_maximum_fusion.2), channel_id=1, source_target_pairs={{4,0},{8,4},{12,8},{16,12},{20,16},{24,20},{28,24},{5,1},{9,5},{13... | collective-permute-start | bytes 221192 | tf_op jit(solution)/shard_map/ppermute | solution.py:347
  6.4 2.0 %shard_map.72.acc_ref = f32[1152,256]{1,0:T(8,128)S(1)} custom-call(s32[1,1,4]{2,1,0:T(1,128)S(1)} %copy-done.3, bf16[8,2,8,2,32,128]{5,4,3,2,1,0:T(8,128)(2,1)S(1)} %bitcast.4, bf16[8,8,32,128]{3,2,1,0:T(8,128)(2,1)S(1)} %copy-done.1), custom_call_target="tpu_custom_call" | custom-call | flops 1207959552 | bytes 2097152 | tf_op jit(solution)/shard_map/pallas_call | solution.py:261
  8.4 3.8 %collective-permute-done.3.gz_ref = bf16[9,32,128]{2,1,0:T(8,128)(2,1)S(1)} collective-permute-done((bf16[9,32,128]{2,1,0:T(8,128)(2,1)S(1)}, bf16[9,32,128]{2,1,0:T(8,128)(2,1)S(1)}, u32[]{:S(2)}, u32[]{:S(2)}) %collective-permute-start.3) | collective-permute-done | bytes 73760 | tf_op jit(solution)/shard_map/ppermute | solution.py:347
  12.2 0.4 shard_map.73
  12.6 1.8 %collective-permute-start.4 = (f32[864,128]{1,0:T(8,128)S(1)}, f32[864,128]{1,0:T(8,128)S(1)}, u32[]{:S(2)}, u32[]{:S(2)}) collective-permute-start(f32[864,128]{1,0:T(8,128)S(1)} %get-tuple-element.14), channel_id=1, source_target_pairs={{0,1},{1,0},{2,3},{3,2},{4,5},{5,4},{6,7},{7,6},{8,9},{9,8},{10,11... | collective-permute-start | bytes 1327112 | tf_op jit(solution)/shard_map/ppermute | solution.py:397
  14.4 1.4 %collective-permute-done.4 = f32[864,128]{1,0:T(8,128)S(1)} collective-permute-done((f32[864,128]{1,0:T(8,128)S(1)}, f32[864,128]{1,0:T(8,128)S(1)}, u32[]{:S(2)}, u32[]{:S(2)}) %collective-permute-start.4) | collective-permute-done | bytes 442400 | tf_op jit(solution)/shard_map/ppermute | solution.py:397
  15.9 3.3 %collective-permute-start.5 = (f32[216,128]{1,0:T(8,128)S(1)}, f32[216,128]{1,0:T(8,128)S(1)}, u32[]{:S(2)}, u32[]{:S(2)}) collective-permute-start(f32[216,128]{1,0:T(8,128)S(1)} %get-tuple-element.17), channel_id=1, source_target_pairs={{0,6},{1,7},{2,4},{3,5},{4,2},{5,3},{6,0},{7,1},{8,14},{9,15},{10,... | collective-permute-start | bytes 331784 | tf_op jit(solution)/shard_map/ppermute | solution.py:397
  19.1 0.7 %collective-permute-start.7 = (f32[216,128]{1,0:T(8,128)S(1)}, f32[216,128]{1,0:T(8,128)S(1)}, u32[]{:S(2)}, u32[]{:S(2)}) collective-permute-start(f32[216,128]{1,0:T(8,128)S(1)} %get-tuple-element.15), channel_id=1, source_target_pairs={{0,2},{1,3},{2,0},{3,1},{4,6},{5,7},{6,4},{7,5},{8,10},{9,11},{10,... | collective-permute-start | bytes 331784 | tf_op jit(solution)/shard_map/ppermute | solution.py:397
  19.8 3.2 %collective-permute-done.5 = f32[216,128]{1,0:T(8,128)S(1)} collective-permute-done((f32[216,128]{1,0:T(8,128)S(1)}, f32[216,128]{1,0:T(8,128)S(1)}, u32[]{:S(2)}, u32[]{:S(2)}) %collective-permute-start.5) | collective-permute-done | bytes 110624 | tf_op jit(solution)/shard_map/ppermute | solution.py:397
  23.0 1.3 %collective-permute-done.6 = f32[216,128]{1,0:T(8,128)S(1)} collective-permute-done((f32[216,128]{1,0:T(8,128)S(1)}, f32[216,128]{1,0:T(8,128)S(1)}, u32[]{:S(2)}, u32[]{:S(2)}) %collective-permute-start.6) | collective-permute-done | bytes 110624 | tf_op jit(solution)/shard_map/ppermute | solution.py:397
  24.3 0.6 collective-permute-done.7
  24.9 1.6 %collective-permute-start.8 = (f32[216,128]{1,0:T(8,128)S(1)}, f32[216,128]{1,0:T(8,128)S(1)}, u32[]{:S(2)}, u32[]{:S(2)}) collective-permute-start(f32[216,128]{1,0:T(8,128)S(1)} %fusion.1), channel_id=1, source_target_pairs={{0,8},{1,9},{2,10},{3,11},{4,12},{5,13},{6,14},{7,15},{8,0},{9,1},... | collective-permute-start | bytes 331784 | tf_op jit(solution)/shard_map/ppermute | solution.py:397
  26.5 1.4 %collective-permute-start = (bf16[16,32,128]{2,1,0:T(8,128)(2,1)S(1)}, bf16[16,32,128]{2,1,0:T(8,128)(2,1)S(1)}, u32[]{:S(2)}, u32[]{:S(2)}) collective-permute-start(bf16[16,32,128]{2,1,0:T(8,128)(2,1)S(1)} %get-tuple-element.9.fy_ref), channel_id=1, source_target_pairs={{0,1},{1,2},{2,3},{4,5},{5,6},{6,7},{8,9},{9,10},{10,11},{12,13},{... | collective-permute-start | bytes 393224 | tf_op jit(solution)/shard_map/ppermute | solution.py:347
  27.9 1.8 %collective-permute-done.8 = f32[216,128]{1,0:T(8,128)S(1)} collective-permute-done((f32[216,128]{1,0:T(8,128)S(1)}, f32[216,128]{1,0:T(8,128)S(1)}, u32[]{:S(2)}, u32[]{:S(2)}) %collective-permute-start.8) | collective-permute-done | bytes 110624 | tf_op jit(solution)/shard_map/ppermute | solution.py:397
  29.7 2.7 %collective-permute-start.9 = (f32[216,128]{1,0:T(8,128)S(1)}, f32[216,128]{1,0:T(8,128)S(1)}, u32[]{:S(2)}, u32[]{:S(2)}) collective-permute-start(f32[216,128]{1,0:T(8,128)S(1)} %add.34), channel_id=1, source_target_pairs={{0,16},{1,17},{2,18},{3,19},{4,20},{5,21},{6,22},{7,23},{8,24},{9,... | collective-permute-start | bytes 331784 | tf_op jit(solution)/shard_map/ppermute | solution.py:397
  32.4 0.0 collective-permute-done.fy_ref
  32.4 5.3 %collective-permute-done.9 = f32[216,128]{1,0:T(8,128)S(1)} collective-permute-done((f32[216,128]{1,0:T(8,128)S(1)}, f32[216,128]{1,0:T(8,128)S(1)}, u32[]{:S(2)}, u32[]{:S(2)}) %collective-permute-start.9) | collective-permute-done | bytes 110624 | tf_op jit(solution)/shard_map/ppermute | solution.py:397
  37.7 2.1 %collective-permute-start.12 = (bf16[216,128]{1,0:T(8,128)(2,1)S(1)}, bf16[216,128]{1,0:T(8,128)(2,1)S(1)}, u32[]{:S(2)}, u32[]{:S(2)}) collective-permute-start(bf16[216,128]{1,0:T(8,128)(2,1)S(1)} %add_convert_fusion.refs_0_), channel_id=1, source_target_pairs={{0,6},{1,7},{2,4},{3,5},{4,2},{5,3},{6,0},{7,1},{8,14},{9,15},{10,... | collective-permute-start | bytes 165896 | tf_op jit(solution)/shard_map/ppermute | solution.py:397
  39.8 0.3 collective-permute-start.11
  40.1 1.4 %collective-permute-start.10 = (bf16[216,128]{1,0:T(8,128)(2,1)S(1)}, bf16[216,128]{1,0:T(8,128)(2,1)S(1)}, u32[]{:S(2)}, u32[]{:S(2)}) collective-permute-start(bf16[216,128]{1,0:T(8,128)(2,1)S(1)} %add_convert_fusion.refs_0_), channel_id=1, source_target_pairs={{0,2},{1,3},{2,0},{3,1},{4,6},{5,7},{6,4},{7,5},{8,10},{9,11},{10,... | collective-permute-start | bytes 165896 | tf_op jit(solution)/shard_map/ppermute | solution.py:397
  41.5 3.9 %collective-permute-start.1 = (bf16[17,32,128]{2,1,0:T(8,128)(2,1)S(1)}, bf16[17,32,128]{2,1,0:T(8,128)(2,1)S(1)}, u32[]{:S(2)}, u32[]{:S(2)}) collective-permute-start(bf16[17,32,128]{2,1,0:T(8,128)(2,1)S(1)} %pad_maximum_fusion.1), channel_id=1, source_target_pairs={{0,4},{4,8},{8,12},{12,16},{16,20},{20,24},{24,28},{1,5},{5,9},{9,... | collective-permute-start | bytes 417800 | tf_op jit(solution)/shard_map/ppermute | solution.py:347
  45.5 0.0 collective-permute-done.12.refs_3_
  45.5 0.1 collective-permute-start.13
  45.6 2.4 %shard_map.68.rest_0_ = bf16[8,8,32,128]{3,2,1,0:T(8,128)(2,1)} custom-call(s32[1,1,4]{2,1,0:T(1,128)S(1)} %copy-done.3, bf16[27,64,128]{2,1,0:T(8,128)(2,1)S(1)} %bitcast.8, bf16[8,2,8,2,32,128]{5,4,3,2,1,0:T(8,128)(2,1)S(1)} %bitcast.5, bf16[8,2,8,2,32,128]{5,4,3,2,1,0:T(8,128)(2,1)S(1)} %bitcast.6, bf16[16,32,128]{2,1,0:T(8,128)(2,1)S(1)} %collective-permute-done.fy_ref), custom_call_target="tpu_custom_call" | custom-call | flops 603979776 | bytes 2097152 | tf_op jit(solution)/shard_map/pallas_call | solution.py:321
  48.0 2.6 %shard_map.70.rest_0_ = bf16[8,2,8,2,32,128]{5,4,3,2,1,0:T(8,128)(2,1)} custom-call(s32[1,1,4]{2,1,0:T(1,128)S(1)} %copy-done.3, bf16[27,64,128]{2,1,0:T(8,128)(2,1)S(1)} %bitcast.9, bf16[8,8,32,128]{3,2,1,0:T(8,128)(2,1)S(1)} %copy-done.1, bf16[9,32,128]{2,1,0:T(8,128)(2,1)S(1)} %collective-permute-done.3.gz_ref, ...), custom_call_target="tpu_custom_call" | custom-call | flops 603979776 | bytes 1048576 | tf_op jit(solution)/shard_map/pallas_call | solution.py:295
  50.7 2.7 %shard_map.71 = bf16[8,2,8,2,32,128]{5,4,3,2,1,0:T(8,128)(2,1)} custom-call(s32[1,1,4]{2,1,0:T(1,128)S(1)} %copy-done.3, bf16[27,64,128]{2,1,0:T(8,128)(2,1)S(1)} %bitcast.10, bf16[8,8,32,128]{3,2,1,0:T(8,128)(2,1)S(1)} %copy-done.1, bf16[9,32,128]{2,1,0:T(8,128)(2,1)S(1)} %collective-permute-done.3.gz_ref, ...), custom_call_target="tpu_custom_call", output_to_operand_aliasing={{}: (5, {})} | custom-call | flops 603979776 | bytes 1048576 | tf_op jit(solution)/shard_map/pallas_call | solution.py:295
  53.4 2.4 %shard_map.69 = bf16[8,8,32,128]{3,2,1,0:T(8,128)(2,1)} custom-call(s32[1,1,4]{2,1,0:T(1,128)S(1)} %copy-done.3, bf16[27,64,128]{2,1,0:T(8,128)(2,1)S(1)} %bitcast.11, bf16[8,2,8,2,32,128]{5,4,3,2,1,0:T(8,128)(2,1)S(1)} %bitcast.7, bf16[17,32,128]{2,1,0:T(8,128)(2,1)S(1)} %collective-permute-done.1.before_ref, ...), custom_call_target="tpu_custom_call", output_to_operand_aliasing={{}: (5, {})} | custom-call | flops 603979776 | bytes 2097152 | tf_op jit(solution)/shard_map/pallas_call | solution.py:321
  55.8 0.8 %shard_map.74.refs_1_ = f32[1728,128]{1,0:T(8,128)} custom-call(bf16[216,128]{1,0:T(8,128)(2,1)S(1)} %add_convert_fusion.refs_0_, bf16[216,128]{1,0:T(8,128)(2,1)S(1)} %collective-permute-done.10.refs_1_, bf16[216,128]{1,0:T(8,128)(2,1)S(1)} %collective-permute-done.11.refs_2_, bf16[216,128]{1,0:T(8,128)(2,1)S(1)} %collective-permute-done.12.refs_3_), custom_call_target="tpu_custom_call" | custom-call | bytes 663552 | tf_op jit(solution)/shard_map/pallas_call | solution.py:379
  56.6 0.8 %shard_map.75 = f32[1728,128]{1,0:T(8,128)} custom-call(bf16[864,128]{1,0:T(8,128)(2,1)S(1)} %collective-permute-done.13.refs_0_, f32[1728,128]{1,0:T(8,128)} %shard_map.74.refs_1_), custom_call_target="tpu_custom_call", output_to_operand_aliasing={{}: (1, {})} | custom-call | bytes 663552 | tf_op jit(solution)/shard_map/pallas_call | solution.py:379
  (22 shorter events, 0.2 us)
Async XLA Ops:
  0.6 5.7 %copy-start.3 = (s32[1,1,4]{2,1,0:T(1,128)S(1)}, s32[1,1,4]{2,1,0:T(1,128)}, u32[]{:S(2)}) copy-start(s32[1,1,4]{2,1,0:T(1,128)} %occ_ref.11) | copy-start | bytes 52
  0.6 5.7 %copy-start = (bf16[16,16,32,128]{3,2,1,0:T(8,128)(2,1)S(1)}, bf16[16,16,32,128]{3,2,1,0:T(8,128)(2,1)}, u32[]{:S(2)}) copy-start(bf16[16,16,32,128]{3,2,1,0:T(8,128)(2,1)} %fb_ref.1) | copy-start | bytes 6291460
  0.7 5.7 %copy-start.1 = (bf16[8,8,32,128]{3,2,1,0:T(8,128)(2,1)S(1)}, bf16[8,8,32,128]{3,2,1,0:T(8,128)(2,1)}, u32[]{:S(2)}) copy-start(bf16[8,8,32,128]{3,2,1,0:T(8,128)(2,1)} %g_ref.5) | copy-start | bytes 1572868
  1.9 3.1 %collective-permute-start.2 = (bf16[8,32,128]{2,1,0:T(8,128)(2,1)S(1)}, bf16[8,32,128]{2,1,0:T(8,128)(2,1)S(1)}, u32[]{:S(2)}, u32[]{:S(2)}) collective-permute-start(bf16[8,32,128]{2,1,0:T(8,128)(2,1)S(1)} %get-tuple-element.12), channel_id=1, source_target_pairs={{1,0},{2,1},{3,2},{5,4},{6,5},{7,6},{9,8},{10,9},{11,10},{13,12},{... | collective-permute-start | bytes 196616 | tf_op jit(solution)/shard_map/ppermute | solution.py:347
  5.0 7.2 %collective-permute-start.3 = (bf16[9,32,128]{2,1,0:T(8,128)(2,1)S(1)}, bf16[9,32,128]{2,1,0:T(8,128)(2,1)S(1)}, u32[]{:S(2)}, u32[]{:S(2)}) collective-permute-start(bf16[9,32,128]{2,1,0:T(8,128)(2,1)S(1)} %pad_maximum_fusion.2), channel_id=1, source_target_pairs={{4,0},{8,4},{12,8},{16,12},{20,16},{24,20},{28,24},{5,1},{9,5},{13... | collective-permute-start | bytes 221192 | tf_op jit(solution)/shard_map/ppermute | solution.py:347
  12.2 33.4 %copy-start.2 = (bf16[3,3,3,64,128]{4,3,2,1,0:T(8,128)(2,1)S(1)}, bf16[3,3,3,64,128]{4,3,2,1,0:T(8,128)(2,1)}, u32[]{:S(2)}) copy-start(bf16[3,3,3,64,128]{4,3,2,1,0:T(8,128)(2,1)} %param.6) | copy-start | bytes 1327108
  12.6 3.2 %collective-permute-start.4 = (f32[864,128]{1,0:T(8,128)S(1)}, f32[864,128]{1,0:T(8,128)S(1)}, u32[]{:S(2)}, u32[]{:S(2)}) collective-permute-start(f32[864,128]{1,0:T(8,128)S(1)} %get-tuple-element.14), channel_id=1, source_target_pairs={{0,1},{1,0},{2,3},{3,2},{4,5},{5,4},{6,7},{7,6},{8,9},{9,8},{10,11... | collective-permute-start | bytes 1327112 | tf_op jit(solution)/shard_map/ppermute | solution.py:397
  15.9 7.2 %collective-permute-start.5 = (f32[216,128]{1,0:T(8,128)S(1)}, f32[216,128]{1,0:T(8,128)S(1)}, u32[]{:S(2)}, u32[]{:S(2)}) collective-permute-start(f32[216,128]{1,0:T(8,128)S(1)} %get-tuple-element.17), channel_id=1, source_target_pairs={{0,6},{1,7},{2,4},{3,5},{4,2},{5,3},{6,0},{7,1},{8,14},{9,15},{10,... | collective-permute-start | bytes 331784 | tf_op jit(solution)/shard_map/ppermute | solution.py:397
  19.1 5.2 %collective-permute-start.6 = (f32[216,128]{1,0:T(8,128)S(1)}, f32[216,128]{1,0:T(8,128)S(1)}, u32[]{:S(2)}, u32[]{:S(2)}) collective-permute-start(f32[216,128]{1,0:T(8,128)S(1)} %get-tuple-element.16), channel_id=1, source_target_pairs={{0,4},{1,5},{2,6},{3,7},{4,0},{5,1},{6,2},{7,3},{8,12},{9,13},{10,... | collective-permute-start | bytes 331784 | tf_op jit(solution)/shard_map/ppermute | solution.py:397
  19.1 5.7 %collective-permute-start.7 = (f32[216,128]{1,0:T(8,128)S(1)}, f32[216,128]{1,0:T(8,128)S(1)}, u32[]{:S(2)}, u32[]{:S(2)}) collective-permute-start(f32[216,128]{1,0:T(8,128)S(1)} %get-tuple-element.15), channel_id=1, source_target_pairs={{0,2},{1,3},{2,0},{3,1},{4,6},{5,7},{6,4},{7,5},{8,10},{9,11},{10,... | collective-permute-start | bytes 331784 | tf_op jit(solution)/shard_map/ppermute | solution.py:397
  24.9 4.8 %collective-permute-start.8 = (f32[216,128]{1,0:T(8,128)S(1)}, f32[216,128]{1,0:T(8,128)S(1)}, u32[]{:S(2)}, u32[]{:S(2)}) collective-permute-start(f32[216,128]{1,0:T(8,128)S(1)} %fusion.1), channel_id=1, source_target_pairs={{0,8},{1,9},{2,10},{3,11},{4,12},{5,13},{6,14},{7,15},{8,0},{9,1},... | collective-permute-start | bytes 331784 | tf_op jit(solution)/shard_map/ppermute | solution.py:397
  26.5 5.8 %collective-permute-start = (bf16[16,32,128]{2,1,0:T(8,128)(2,1)S(1)}, bf16[16,32,128]{2,1,0:T(8,128)(2,1)S(1)}, u32[]{:S(2)}, u32[]{:S(2)}) collective-permute-start(bf16[16,32,128]{2,1,0:T(8,128)(2,1)S(1)} %get-tuple-element.9.fy_ref), channel_id=1, source_target_pairs={{0,1},{1,2},{2,3},{4,5},{5,6},{6,7},{8,9},{9,10},{10,11},{12,13},{... | collective-permute-start | bytes 393224 | tf_op jit(solution)/shard_map/ppermute | solution.py:347
  29.7 7.9 %collective-permute-start.9 = (f32[216,128]{1,0:T(8,128)S(1)}, f32[216,128]{1,0:T(8,128)S(1)}, u32[]{:S(2)}, u32[]{:S(2)}) collective-permute-start(f32[216,128]{1,0:T(8,128)S(1)} %add.34), channel_id=1, source_target_pairs={{0,16},{1,17},{2,18},{3,19},{4,20},{5,21},{6,22},{7,23},{8,24},{9,... | collective-permute-start | bytes 331784 | tf_op jit(solution)/shard_map/ppermute | solution.py:397
  37.7 7.8 %collective-permute-start.12 = (bf16[216,128]{1,0:T(8,128)(2,1)S(1)}, bf16[216,128]{1,0:T(8,128)(2,1)S(1)}, u32[]{:S(2)}, u32[]{:S(2)}) collective-permute-start(bf16[216,128]{1,0:T(8,128)(2,1)S(1)} %add_convert_fusion.refs_0_), channel_id=1, source_target_pairs={{0,6},{1,7},{2,4},{3,5},{4,2},{5,3},{6,0},{7,1},{8,14},{9,15},{10,... | collective-permute-start | bytes 165896 | tf_op jit(solution)/shard_map/ppermute | solution.py:397
  39.8 5.7 %collective-permute-start.11 = (bf16[216,128]{1,0:T(8,128)(2,1)S(1)}, bf16[216,128]{1,0:T(8,128)(2,1)S(1)}, u32[]{:S(2)}, u32[]{:S(2)}) collective-permute-start(bf16[216,128]{1,0:T(8,128)(2,1)S(1)} %add_convert_fusion.refs_0_), channel_id=1, source_target_pairs={{0,4},{1,5},{2,6},{3,7},{4,0},{5,1},{6,2},{7,3},{8,12},{9,13},{10,... | collective-permute-start | bytes 165896 | tf_op jit(solution)/shard_map/ppermute | solution.py:397
  40.1 5.4 %collective-permute-start.10 = (bf16[216,128]{1,0:T(8,128)(2,1)S(1)}, bf16[216,128]{1,0:T(8,128)(2,1)S(1)}, u32[]{:S(2)}, u32[]{:S(2)}) collective-permute-start(bf16[216,128]{1,0:T(8,128)(2,1)S(1)} %add_convert_fusion.refs_0_), channel_id=1, source_target_pairs={{0,2},{1,3},{2,0},{3,1},{4,6},{5,7},{6,4},{7,5},{8,10},{9,11},{10,... | collective-permute-start | bytes 165896 | tf_op jit(solution)/shard_map/ppermute | solution.py:397
  41.5 11.8 %collective-permute-start.1 = (bf16[17,32,128]{2,1,0:T(8,128)(2,1)S(1)}, bf16[17,32,128]{2,1,0:T(8,128)(2,1)S(1)}, u32[]{:S(2)}, u32[]{:S(2)}) collective-permute-start(bf16[17,32,128]{2,1,0:T(8,128)(2,1)S(1)} %pad_maximum_fusion.1), channel_id=1, source_target_pairs={{0,4},{4,8},{8,12},{12,16},{16,20},{20,24},{24,28},{1,5},{5,9},{9,... | collective-permute-start | bytes 417800 | tf_op jit(solution)/shard_map/ppermute | solution.py:347
  45.5 11.0 %collective-permute-start.13 = (bf16[864,128]{1,0:T(8,128)(2,1)S(1)}, bf16[864,128]{1,0:T(8,128)(2,1)S(1)}, u32[]{:S(2)}, u32[]{:S(2)}) collective-permute-start(bf16[864,128]{1,0:T(8,128)(2,1)S(1)} %pad_maximum_fusion), channel_id=1, source_target_pairs={{0,1},{1,0},{2,3},{3,2},{4,5},{5,4},{6,7},{7,6},{8,9},{9,8},{10,11... | collective-permute-start | bytes 663560 | tf_op jit(solution)/shard_map/ppermute | solution.py:397

commit v3 on v2

--- a/solution.py
+++ b/solution.py
@@ -285,7 +285,7 @@
     )(acc, fz, fy, gz, gy)
 
 
-def data_grad(occ, kernel, grad, gz, gy, first, count, into=None, na=2):
+def data_grad(occ, kernel, grad, gz, gy, first, count, into=None, na=4):
     zo, yo, pairs, cout = grad.shape
     cin = kernel.shape[1]
     chans = 2 * cin
@@ -435,9 +435,9 @@
 
     fy = shifted(ry, "gy", 1)
     fz = shifted(jnp.concatenate([fy[-1:], rz], 0), "gz", 1)
-    mid = zo // 2
-    coarse = coarse_conv(occupancy, taps, split, split, fy, mid, zo - mid)
-    coarse = coarse_conv(occupancy, taps, split, fz, fy, 0, mid, coarse)
+    mid, late = zo // 2, zo - zo // 4
+    coarse = coarse_conv(occupancy, taps, split, split, fy, late, zo - late)
+    coarse = coarse_conv(occupancy, taps, split, fz, fy, 0, late, coarse, na=3)
     given = (occupancy, taps, upstream, gz, gy)
     low = data_grad(*given, 0, mid)
     feature_grad = data_grad(*given, mid, zo - mid, low).reshape(features.shape)

time: 57.6 us -> 56.9 us (0.988)
  Pallas kernels: 15.3 us -> 14.6 us
  transfers between devices with their start and end apart: 14 -> 14, of which waited for: 8 -> 8; matrix products, arithmetic and copies ran while one was open for 0% -> 0% of each run, Pallas kernels for 23% -> 22%
where the time goes in v3:
time: 56.9 us; the launch traced here: 56.7 us
  starting transfers between devices  21.8 us (38%)
  waiting for transfers between devices  19.3 us (34%)
  Pallas kernels  14.6 us (26%)
  between operations  0.83 us (1%)
    ppermute x10, starting transfers between devices, hop(): lax.ppermute(x, both, partners(nz, ny, lambda z, y: (z ^ flip_z, y ^ flip...  13.9 us
    ppermute x10, waiting for transfers between devices, hop(): lax.ppermute(x, both, partners(nz, ny, lambda z, y: (z ^ flip_z, y ^ flip...  13.6 us
    ppermute x4, starting transfers between devices, shifted(): lax.ppermute(block, axis, [(i, i + distance) for i in range(n) if 0 <= i...  7.88 us
    ppermute x4, waiting for transfers between devices, shifted(): lax.ppermute(block, axis, [(i, i + distance) for i in range(n) if 0 <= i...  5.69 us
    pallas_call x2, Pallas kernels, data_grad(): pl.pallas_call(functools.partial(data_kernel, first=first), grid=(count /...  4.89 us
    pallas_call x2, Pallas kernels, coarse_conv(): pl.pallas_call(functools.partial(coarse_kernel, first=first), grid=(count...  4.51 us
    pallas_call x1, Pallas kernels, weight_grad(): pl.pallas_call(weight_kernel, in_specs=[SCALARS, vmem, vmem], out_specs=v...  2.02 us
    pallas_call x2, Pallas kernels, joined(): pl.pallas_call(functools.partial(join_kernel, other=other), in_specs=[pl....  1.62 us
  transfers between devices with their start and end apart: 14, of which 8 were waited for; matrix products, arithmetic and copies ran while one was open for 0% of the time, Pallas kernels for 22%

profile of v3, /device:TPU:0, one launch (start us, length us, event | category | flops | bytes accessed | tf_op | source)
XLA Modules:
  0.0 56.7 jit_solution(2521479411091574638)
XLA Ops:
  0.7 1.2 %shard_map.67 = (bf16[8,32,128]{2,1,0:T(8,128)(2,1)S(1)}, bf16[8,32,128]{2,1,0:T(8,128)(2,1)S(1)}, bf16[16,32,128]{2,1,0:T(8,128)(2,1)S(1)}, bf16[16,32,128]{2,1,0:T(8,128)(2,1)S(1)}) custom-call(s32[1,1,4]{2,1,0:T(1,128)} %occ_ref.11, bf16[16,16,32,128]{3,2,1,0:T(8,128)(2,1)} %fb_ref.1, bf16[16,16,32,128]{3,2,1,0:T(8,128)(2,1)} %fb_ref.1, ...), custom_call_target="tpu_custom_call" | custom-call | bytes 786432 | tf_op jit(solution)/shard_map/pallas_call | solution.py:63
  1.9 1.3 %collective-permute-start.2 = (bf16[8,32,128]{2,1,0:T(8,128)(2,1)S(1)}, bf16[8,32,128]{2,1,0:T(8,128)(2,1)S(1)}, u32[]{:S(2)}, u32[]{:S(2)}) collective-permute-start(bf16[8,32,128]{2,1,0:T(8,128)(2,1)S(1)} %get-tuple-element.12), channel_id=1, source_target_pairs={{1,0},{2,1},{3,2},{5,4},{6,5},{7,6},{9,8},{10,9},{11,10},{13,12},{... | collective-permute-start | bytes 196616 | tf_op jit(solution)/shard_map/ppermute | solution.py:347
  3.2 1.8 %collective-permute-done.2.gy_ref = bf16[8,32,128]{2,1,0:T(8,128)(2,1)S(1)} collective-permute-done((bf16[8,32,128]{2,1,0:T(8,128)(2,1)S(1)}, bf16[8,32,128]{2,1,0:T(8,128)(2,1)S(1)}, u32[]{:S(2)}, u32[]{:S(2)}) %collective-permute-start.2) | collective-permute-done | bytes 65568 | tf_op jit(solution)/shard_map/ppermute | solution.py:347
  5.0 1.3 %collective-permute-start.3 = (bf16[9,32,128]{2,1,0:T(8,128)(2,1)S(1)}, bf16[9,32,128]{2,1,0:T(8,128)(2,1)S(1)}, u32[]{:S(2)}, u32[]{:S(2)}) collective-permute-start(bf16[9,32,128]{2,1,0:T(8,128)(2,1)S(1)} %pad_maximum_fusion.2), channel_id=1, source_target_pairs={{4,0},{8,4},{12,8},{16,12},{20,16},{24,20},{28,24},{5,1},{9,5},{13... | collective-permute-start | bytes 221192 | tf_op jit(solution)/shard_map/ppermute | solution.py:347
  6.4 2.0 %shard_map.72.acc_ref = f32[1152,256]{1,0:T(8,128)S(1)} custom-call(s32[1,1,4]{2,1,0:T(1,128)S(1)} %copy-done.3, bf16[8,2,8,2,32,128]{5,4,3,2,1,0:T(8,128)(2,1)S(1)} %bitcast.4, bf16[8,8,32,128]{3,2,1,0:T(8,128)(2,1)S(1)} %copy-done.1), custom_call_target="tpu_custom_call" | custom-call | flops 1207959552 | bytes 2097152 | tf_op jit(solution)/shard_map/pallas_call | solution.py:261
  8.4 3.8 %collective-permute-done.3.gz_ref = bf16[9,32,128]{2,1,0:T(8,128)(2,1)S(1)} collective-permute-done((bf16[9,32,128]{2,1,0:T(8,128)(2,1)S(1)}, bf16[9,32,128]{2,1,0:T(8,128)(2,1)S(1)}, u32[]{:S(2)}, u32[]{:S(2)}) %collective-permute-start.3) | collective-permute-done | bytes 73760 | tf_op jit(solution)/shard_map/ppermute | solution.py:347
  12.2 0.4 shard_map.73
  12.6 1.8 %collective-permute-start.4 = (f32[864,128]{1,0:T(8,128)S(1)}, f32[864,128]{1,0:T(8,128)S(1)}, u32[]{:S(2)}, u32[]{:S(2)}) collective-permute-start(f32[864,128]{1,0:T(8,128)S(1)} %get-tuple-element.14), channel_id=1, source_target_pairs={{0,1},{1,0},{2,3},{3,2},{4,5},{5,4},{6,7},{7,6},{8,9},{9,8},{10,11... | collective-permute-start | bytes 1327112 | tf_op jit(solution)/shard_map/ppermute | solution.py:397
  14.4 1.4 %collective-permute-done.4 = f32[864,128]{1,0:T(8,128)S(1)} collective-permute-done((f32[864,128]{1,0:T(8,128)S(1)}, f32[864,128]{1,0:T(8,128)S(1)}, u32[]{:S(2)}, u32[]{:S(2)}) %collective-permute-start.4) | collective-permute-done | bytes 442400 | tf_op jit(solution)/shard_map/ppermute | solution.py:397
  15.9 3.3 %collective-permute-start.5 = (f32[216,128]{1,0:T(8,128)S(1)}, f32[216,128]{1,0:T(8,128)S(1)}, u32[]{:S(2)}, u32[]{:S(2)}) collective-permute-start(f32[216,128]{1,0:T(8,128)S(1)} %get-tuple-element.17), channel_id=1, source_target_pairs={{0,6},{1,7},{2,4},{3,5},{4,2},{5,3},{6,0},{7,1},{8,14},{9,15},{10,... | collective-permute-start | bytes 331784 | tf_op jit(solution)/shard_map/ppermute | solution.py:397
  19.1 0.7 %collective-permute-start.7 = (f32[216,128]{1,0:T(8,128)S(1)}, f32[216,128]{1,0:T(8,128)S(1)}, u32[]{:S(2)}, u32[]{:S(2)}) collective-permute-start(f32[216,128]{1,0:T(8,128)S(1)} %get-tuple-element.15), channel_id=1, source_target_pairs={{0,2},{1,3},{2,0},{3,1},{4,6},{5,7},{6,4},{7,5},{8,10},{9,11},{10,... | collective-permute-start | bytes 331784 | tf_op jit(solution)/shard_map/ppermute | solution.py:397
  19.8 3.2 %collective-permute-done.5 = f32[216,128]{1,0:T(8,128)S(1)} collective-permute-done((f32[216,128]{1,0:T(8,128)S(1)}, f32[216,128]{1,0:T(8,128)S(1)}, u32[]{:S(2)}, u32[]{:S(2)}) %collective-permute-start.5) | collective-permute-done | bytes 110624 | tf_op jit(solution)/shard_map/ppermute | solution.py:397
  23.0 1.3 %collective-permute-done.6 = f32[216,128]{1,0:T(8,128)S(1)} collective-permute-done((f32[216,128]{1,0:T(8,128)S(1)}, f32[216,128]{1,0:T(8,128)S(1)}, u32[]{:S(2)}, u32[]{:S(2)}) %collective-permute-start.6) | collective-permute-done | bytes 110624 | tf_op jit(solution)/shard_map/ppermute | solution.py:397
  24.3 0.6 collective-permute-done.7
  24.9 1.6 %collective-permute-start.8 = (f32[216,128]{1,0:T(8,128)S(1)}, f32[216,128]{1,0:T(8,128)S(1)}, u32[]{:S(2)}, u32[]{:S(2)}) collective-permute-start(f32[216,128]{1,0:T(8,128)S(1)} %fusion.1), channel_id=1, source_target_pairs={{0,8},{1,9},{2,10},{3,11},{4,12},{5,13},{6,14},{7,15},{8,0},{9,1},... | collective-permute-start | bytes 331784 | tf_op jit(solution)/shard_map/ppermute | solution.py:397
  26.5 1.4 %collective-permute-start = (bf16[16,32,128]{2,1,0:T(8,128)(2,1)S(1)}, bf16[16,32,128]{2,1,0:T(8,128)(2,1)S(1)}, u32[]{:S(2)}, u32[]{:S(2)}) collective-permute-start(bf16[16,32,128]{2,1,0:T(8,128)(2,1)S(1)} %get-tuple-element.9.fy_ref), channel_id=1, source_target_pairs={{0,1},{1,2},{2,3},{4,5},{5,6},{6,7},{8,9},{9,10},{10,11},{12,13},{... | collective-permute-start | bytes 393224 | tf_op jit(solution)/shard_map/ppermute | solution.py:347
  27.9 1.8 %collective-permute-done.8 = f32[216,128]{1,0:T(8,128)S(1)} collective-permute-done((f32[216,128]{1,0:T(8,128)S(1)}, f32[216,128]{1,0:T(8,128)S(1)}, u32[]{:S(2)}, u32[]{:S(2)}) %collective-permute-start.8) | collective-permute-done | bytes 110624 | tf_op jit(solution)/shard_map/ppermute | solution.py:397
  29.7 2.7 %collective-permute-start.9 = (f32[216,128]{1,0:T(8,128)S(1)}, f32[216,128]{1,0:T(8,128)S(1)}, u32[]{:S(2)}, u32[]{:S(2)}) collective-permute-start(f32[216,128]{1,0:T(8,128)S(1)} %add.34), channel_id=1, source_target_pairs={{0,16},{1,17},{2,18},{3,19},{4,20},{5,21},{6,22},{7,23},{8,24},{9,... | collective-permute-start | bytes 331784 | tf_op jit(solution)/shard_map/ppermute | solution.py:397
  32.4 0.0 collective-permute-done.fy_ref
  32.4 5.3 %collective-permute-done.9 = f32[216,128]{1,0:T(8,128)S(1)} collective-permute-done((f32[216,128]{1,0:T(8,128)S(1)}, f32[216,128]{1,0:T(8,128)S(1)}, u32[]{:S(2)}, u32[]{:S(2)}) %collective-permute-start.9) | collective-permute-done | bytes 110624 | tf_op jit(solution)/shard_map/ppermute | solution.py:397
  37.7 2.1 %collective-permute-start.12 = (bf16[216,128]{1,0:T(8,128)(2,1)S(1)}, bf16[216,128]{1,0:T(8,128)(2,1)S(1)}, u32[]{:S(2)}, u32[]{:S(2)}) collective-permute-start(bf16[216,128]{1,0:T(8,128)(2,1)S(1)} %add_convert_fusion.refs_0_), channel_id=1, source_target_pairs={{0,6},{1,7},{2,4},{3,5},{4,2},{5,3},{6,0},{7,1},{8,14},{9,15},{10,... | collective-permute-start | bytes 165896 | tf_op jit(solution)/shard_map/ppermute | solution.py:397
  39.8 0.3 collective-permute-start.11
  40.1 1.4 %collective-permute-start.10 = (bf16[216,128]{1,0:T(8,128)(2,1)S(1)}, bf16[216,128]{1,0:T(8,128)(2,1)S(1)}, u32[]{:S(2)}, u32[]{:S(2)}) collective-permute-start(bf16[216,128]{1,0:T(8,128)(2,1)S(1)} %add_convert_fusion.refs_0_), channel_id=1, source_target_pairs={{0,2},{1,3},{2,0},{3,1},{4,6},{5,7},{6,4},{7,5},{8,10},{9,11},{10,... | collective-permute-start | bytes 165896 | tf_op jit(solution)/shard_map/ppermute | solution.py:397
  41.5 3.9 %collective-permute-start.1 = (bf16[17,32,128]{2,1,0:T(8,128)(2,1)S(1)}, bf16[17,32,128]{2,1,0:T(8,128)(2,1)S(1)}, u32[]{:S(2)}, u32[]{:S(2)}) collective-permute-start(bf16[17,32,128]{2,1,0:T(8,128)(2,1)S(1)} %pad_maximum_fusion.1), channel_id=1, source_target_pairs={{0,4},{4,8},{8,12},{12,16},{16,20},{20,24},{24,28},{1,5},{5,9},{9,... | collective-permute-start | bytes 417800 | tf_op jit(solution)/shard_map/ppermute | solution.py:347
  45.5 0.0 collective-permute-done.12.refs_3_
  45.5 0.1 collective-permute-start.13
  45.6 1.8 %shard_map.68.rest_0_ = bf16[8,8,32,128]{3,2,1,0:T(8,128)(2,1)} custom-call(s32[1,1,4]{2,1,0:T(1,128)S(1)} %copy-done.3, bf16[27,64,128]{2,1,0:T(8,128)(2,1)S(1)} %bitcast.8, bf16[8,2,8,2,32,128]{5,4,3,2,1,0:T(8,128)(2,1)S(1)} %bitcast.5, bf16[8,2,8,2,32,128]{5,4,3,2,1,0:T(8,128)(2,1)S(1)} %bitcast.6, bf16[16,32,128]{2,1,0:T(8,128)(2,1)S(1)} %collective-permute-done.fy_ref), custom_call_target="tpu_custom_call" | custom-call | flops 301989888 | bytes 2097152 | tf_op jit(solution)/shard_map/pallas_call | solution.py:321
  47.4 2.4 %shard_map.70.rest_0_ = bf16[8,2,8,2,32,128]{5,4,3,2,1,0:T(8,128)(2,1)} custom-call(s32[1,1,4]{2,1,0:T(1,128)S(1)} %copy-done.3, bf16[27,64,128]{2,1,0:T(8,128)(2,1)S(1)} %bitcast.9, bf16[8,8,32,128]{3,2,1,0:T(8,128)(2,1)S(1)} %copy-done.1, bf16[9,32,128]{2,1,0:T(8,128)(2,1)S(1)} %collective-permute-done.3.gz_ref, ...), custom_call_target="tpu_custom_call" | custom-call | flops 603979776 | bytes 1048576 | tf_op jit(solution)/shard_map/pallas_call | solution.py:295
  49.9 2.4 %shard_map.71 = bf16[8,2,8,2,32,128]{5,4,3,2,1,0:T(8,128)(2,1)} custom-call(s32[1,1,4]{2,1,0:T(1,128)S(1)} %copy-done.3, bf16[27,64,128]{2,1,0:T(8,128)(2,1)S(1)} %bitcast.10, bf16[8,8,32,128]{3,2,1,0:T(8,128)(2,1)S(1)} %copy-done.1, bf16[9,32,128]{2,1,0:T(8,128)(2,1)S(1)} %collective-permute-done.3.gz_ref, ...), custom_call_target="tpu_custom_call", output_to_operand_aliasing={{}: (5, {})} | custom-call | flops 603979776 | bytes 1048576 | tf_op jit(solution)/shard_map/pallas_call | solution.py:295
  52.3 2.7 %shard_map.69 = bf16[8,8,32,128]{3,2,1,0:T(8,128)(2,1)} custom-call(s32[1,1,4]{2,1,0:T(1,128)S(1)} %copy-done.3, bf16[27,64,128]{2,1,0:T(8,128)(2,1)S(1)} %bitcast.11, bf16[8,2,8,2,32,128]{5,4,3,2,1,0:T(8,128)(2,1)S(1)} %bitcast.7, bf16[17,32,128]{2,1,0:T(8,128)(2,1)S(1)} %collective-permute-done.1.before_ref, ...), custom_call_target="tpu_custom_call", output_to_operand_aliasing={{}: (5, {})} | custom-call | flops 905969664 | bytes 2097152 | tf_op jit(solution)/shard_map/pallas_call | solution.py:321
  55.0 0.8 %shard_map.74.refs_1_ = f32[1728,128]{1,0:T(8,128)} custom-call(bf16[216,128]{1,0:T(8,128)(2,1)S(1)} %add_convert_fusion.refs_0_, bf16[216,128]{1,0:T(8,128)(2,1)S(1)} %collective-permute-done.10.refs_1_, bf16[216,128]{1,0:T(8,128)(2,1)S(1)} %collective-permute-done.11.refs_2_, bf16[216,128]{1,0:T(8,128)(2,1)S(1)} %collective-permute-done.12.refs_3_), custom_call_target="tpu_custom_call" | custom-call | bytes 663552 | tf_op jit(solution)/shard_map/pallas_call | solution.py:379
  55.9 0.8 %shard_map.75 = f32[1728,128]{1,0:T(8,128)} custom-call(bf16[864,128]{1,0:T(8,128)(2,1)S(1)} %collective-permute-done.13.refs_0_, f32[1728,128]{1,0:T(8,128)} %shard_map.74.refs_1_), custom_call_target="tpu_custom_call", output_to_operand_aliasing={{}: (1, {})} | custom-call | bytes 663552 | tf_op jit(solution)/shard_map/pallas_call | solution.py:379
  (22 shorter events, 0.2 us)
Async XLA Ops:
  0.6 5.7 %copy-start.3 = (s32[1,1,4]{2,1,0:T(1,128)S(1)}, s32[1,1,4]{2,1,0:T(1,128)}, u32[]{:S(2)}) copy-start(s32[1,1,4]{2,1,0:T(1,128)} %occ_ref.11) | copy-start | bytes 52
  0.6 5.7 %copy-start = (bf16[16,16,32,128]{3,2,1,0:T(8,128)(2,1)S(1)}, bf16[16,16,32,128]{3,2,1,0:T(8,128)(2,1)}, u32[]{:S(2)}) copy-start(bf16[16,16,32,128]{3,2,1,0:T(8,128)(2,1)} %fb_ref.1) | copy-start | bytes 6291460
  0.7 5.7 %copy-start.1 = (bf16[8,8,32,128]{3,2,1,0:T(8,128)(2,1)S(1)}, bf16[8,8,32,128]{3,2,1,0:T(8,128)(2,1)}, u32[]{:S(2)}) copy-start(bf16[8,8,32,128]{3,2,1,0:T(8,128)(2,1)} %g_ref.5) | copy-start | bytes 1572868
  1.9 3.1 %collective-permute-start.2 = (bf16[8,32,128]{2,1,0:T(8,128)(2,1)S(1)}, bf16[8,32,128]{2,1,0:T(8,128)(2,1)S(1)}, u32[]{:S(2)}, u32[]{:S(2)}) collective-permute-start(bf16[8,32,128]{2,1,0:T(8,128)(2,1)S(1)} %get-tuple-element.12), channel_id=1, source_target_pairs={{1,0},{2,1},{3,2},{5,4},{6,5},{7,6},{9,8},{10,9},{11,10},{13,12},{... | collective-permute-start | bytes 196616 | tf_op jit(solution)/shard_map/ppermute | solution.py:347
  5.0 7.2 %collective-permute-start.3 = (bf16[9,32,128]{2,1,0:T(8,128)(2,1)S(1)}, bf16[9,32,128]{2,1,0:T(8,128)(2,1)S(1)}, u32[]{:S(2)}, u32[]{:S(2)}) collective-permute-start(bf16[9,32,128]{2,1,0:T(8,128)(2,1)S(1)} %pad_maximum_fusion.2), channel_id=1, source_target_pairs={{4,0},{8,4},{12,8},{16,12},{20,16},{24,20},{28,24},{5,1},{9,5},{13... | collective-permute-start | bytes 221192 | tf_op jit(solution)/shard_map/ppermute | solution.py:347
  12.2 33.4 %copy-start.2 = (bf16[3,3,3,64,128]{4,3,2,1,0:T(8,128)(2,1)S(1)}, bf16[3,3,3,64,128]{4,3,2,1,0:T(8,128)(2,1)}, u32[]{:S(2)}) copy-start(bf16[3,3,3,64,128]{4,3,2,1,0:T(8,128)(2,1)} %param.6) | copy-start | bytes 1327108
  12.6 3.2 %collective-permute-start.4 = (f32[864,128]{1,0:T(8,128)S(1)}, f32[864,128]{1,0:T(8,128)S(1)}, u32[]{:S(2)}, u32[]{:S(2)}) collective-permute-start(f32[864,128]{1,0:T(8,128)S(1)} %get-tuple-element.14), channel_id=1, source_target_pairs={{0,1},{1,0},{2,3},{3,2},{4,5},{5,4},{6,7},{7,6},{8,9},{9,8},{10,11... | collective-permute-start | bytes 1327112 | tf_op jit(solution)/shard_map/ppermute | solution.py:397
  15.9 7.2 %collective-permute-start.5 = (f32[216,128]{1,0:T(8,128)S(1)}, f32[216,128]{1,0:T(8,128)S(1)}, u32[]{:S(2)}, u32[]{:S(2)}) collective-permute-start(f32[216,128]{1,0:T(8,128)S(1)} %get-tuple-element.17), channel_id=1, source_target_pairs={{0,6},{1,7},{2,4},{3,5},{4,2},{5,3},{6,0},{7,1},{8,14},{9,15},{10,... | collective-permute-start | bytes 331784 | tf_op jit(solution)/shard_map/ppermute | solution.py:397
  19.1 5.2 %collective-permute-start.6 = (f32[216,128]{1,0:T(8,128)S(1)}, f32[216,128]{1,0:T(8,128)S(1)}, u32[]{:S(2)}, u32[]{:S(2)}) collective-permute-start(f32[216,128]{1,0:T(8,128)S(1)} %get-tuple-element.16), channel_id=1, source_target_pairs={{0,4},{1,5},{2,6},{3,7},{4,0},{5,1},{6,2},{7,3},{8,12},{9,13},{10,... | collective-permute-start | bytes 331784 | tf_op jit(solution)/shard_map/ppermute | solution.py:397
  19.1 5.7 %collective-permute-start.7 = (f32[216,128]{1,0:T(8,128)S(1)}, f32[216,128]{1,0:T(8,128)S(1)}, u32[]{:S(2)}, u32[]{:S(2)}) collective-permute-start(f32[216,128]{1,0:T(8,128)S(1)} %get-tuple-element.15), channel_id=1, source_target_pairs={{0,2},{1,3},{2,0},{3,1},{4,6},{5,7},{6,4},{7,5},{8,10},{9,11},{10,... | collective-permute-start | bytes 331784 | tf_op jit(solution)/shard_map/ppermute | solution.py:397
  24.9 4.8 %collective-permute-start.8 = (f32[216,128]{1,0:T(8,128)S(1)}, f32[216,128]{1,0:T(8,128)S(1)}, u32[]{:S(2)}, u32[]{:S(2)}) collective-permute-start(f32[216,128]{1,0:T(8,128)S(1)} %fusion.1), channel_id=1, source_target_pairs={{0,8},{1,9},{2,10},{3,11},{4,12},{5,13},{6,14},{7,15},{8,0},{9,1},... | collective-permute-start | bytes 331784 | tf_op jit(solution)/shard_map/ppermute | solution.py:397
  26.5 5.8 %collective-permute-start = (bf16[16,32,128]{2,1,0:T(8,128)(2,1)S(1)}, bf16[16,32,128]{2,1,0:T(8,128)(2,1)S(1)}, u32[]{:S(2)}, u32[]{:S(2)}) collective-permute-start(bf16[16,32,128]{2,1,0:T(8,128)(2,1)S(1)} %get-tuple-element.9.fy_ref), channel_id=1, source_target_pairs={{0,1},{1,2},{2,3},{4,5},{5,6},{6,7},{8,9},{9,10},{10,11},{12,13},{... | collective-permute-start | bytes 393224 | tf_op jit(solution)/shard_map/ppermute | solution.py:347
  29.7 7.9 %collective-permute-start.9 = (f32[216,128]{1,0:T(8,128)S(1)}, f32[216,128]{1,0:T(8,128)S(1)}, u32[]{:S(2)}, u32[]{:S(2)}) collective-permute-start(f32[216,128]{1,0:T(8,128)S(1)} %add.34), channel_id=1, source_target_pairs={{0,16},{1,17},{2,18},{3,19},{4,20},{5,21},{6,22},{7,23},{8,24},{9,... | collective-permute-start | bytes 331784 | tf_op jit(solution)/shard_map/ppermute | solution.py:397
  37.7 7.8 %collective-permute-start.12 = (bf16[216,128]{1,0:T(8,128)(2,1)S(1)}, bf16[216,128]{1,0:T(8,128)(2,1)S(1)}, u32[]{:S(2)}, u32[]{:S(2)}) collective-permute-start(bf16[216,128]{1,0:T(8,128)(2,1)S(1)} %add_convert_fusion.refs_0_), channel_id=1, source_target_pairs={{0,6},{1,7},{2,4},{3,5},{4,2},{5,3},{6,0},{7,1},{8,14},{9,15},{10,... | collective-permute-start | bytes 165896 | tf_op jit(solution)/shard_map/ppermute | solution.py:397
  39.8 5.7 %collective-permute-start.11 = (bf16[216,128]{1,0:T(8,128)(2,1)S(1)}, bf16[216,128]{1,0:T(8,128)(2,1)S(1)}, u32[]{:S(2)}, u32[]{:S(2)}) collective-permute-start(bf16[216,128]{1,0:T(8,128)(2,1)S(1)} %add_convert_fusion.refs_0_), channel_id=1, source_target_pairs={{0,4},{1,5},{2,6},{3,7},{4,0},{5,1},{6,2},{7,3},{8,12},{9,13},{10,... | collective-permute-start | bytes 165896 | tf_op jit(solution)/shard_map/ppermute | solution.py:397
  40.1 5.4 %collective-permute-start.10 = (bf16[216,128]{1,0:T(8,128)(2,1)S(1)}, bf16[216,128]{1,0:T(8,128)(2,1)S(1)}, u32[]{:S(2)}, u32[]{:S(2)}) collective-permute-start(bf16[216,128]{1,0:T(8,128)(2,1)S(1)} %add_convert_fusion.refs_0_), channel_id=1, source_target_pairs={{0,2},{1,3},{2,0},{3,1},{4,6},{5,7},{6,4},{7,5},{8,10},{9,11},{10,... | collective-permute-start | bytes 165896 | tf_op jit(solution)/shard_map/ppermute | solution.py:397
  41.5 10.8 %collective-permute-start.1 = (bf16[17,32,128]{2,1,0:T(8,128)(2,1)S(1)}, bf16[17,32,128]{2,1,0:T(8,128)(2,1)S(1)}, u32[]{:S(2)}, u32[]{:S(2)}) collective-permute-start(bf16[17,32,128]{2,1,0:T(8,128)(2,1)S(1)} %pad_maximum_fusion.1), channel_id=1, source_target_pairs={{0,4},{4,8},{8,12},{12,16},{16,20},{20,24},{24,28},{1,5},{5,9},{9,... | collective-permute-start | bytes 417800 | tf_op jit(solution)/shard_map/ppermute | solution.py:347
  45.5 10.3 %collective-permute-start.13 = (bf16[864,128]{1,0:T(8,128)(2,1)S(1)}, bf16[864,128]{1,0:T(8,128)(2,1)S(1)}, u32[]{:S(2)}, u32[]{:S(2)}) collective-permute-start(bf16[864,128]{1,0:T(8,128)(2,1)S(1)} %pad_maximum_fusion), channel_id=1, source_target_pairs={{0,1},{1,0},{2,3},{3,2},{4,5},{5,4},{6,7},{7,6},{8,9},{9,8},{10,11... | collective-permute-start | bytes 663560 | tf_op jit(solution)/shard_map/ppermute | solution.py:397
